TPU v7x, 128 devices: a whole 4x4x4 slice. The times are simulated.
128 devices in a mesh: src: 8 (over z, core), tgt: 16 (over y, x).
Axes of the slice: x: 4, y: 4, z: 4, core: 2. Of those that a mesh axis runs over, the one named last changes fastest.
Arguments:
- source: bfloat16 [16384, 512], P(('src', 'tgt')), may hold values from -64 to 64
- target: bfloat16 [16384, 512], P('tgt', 'src'), may hold values from -64 to 64
- rotation: float32 [512, 512], replicated, may hold values from -0.06 to 1.06
Outputs:
- aligned: float32 [512, 512], replicated
- moved: float32 [16384, 512], P(('src', 'tgt'))
All inputs are finite; a program needn't handle non-finite values.
Results may differ from a plain program's by a relative error of at most 0.013.
Values may be sent and summed in bfloat16 or wider, within the bound.
A program may use at most 64 MiB of HBM per device.

v0:
```python
import functools
import math

import jax
import jax.numpy as jnp
from jax import lax
from jax.experimental import pallas as pl
from jax.experimental.pallas import tpu as pltpu
from jax.sharding import PartitionSpec as P

ROUNDS = 2
MESH = pl.DeviceIdType.MESH
F32, BF16 = jnp.float32, jnp.bfloat16
NSRC, NTGT = 8, 16
D = 512
OWN = 128
ROWS = 2048
COLS = 1024
CH = 256
RB = 32
LOG_N = 14.0
SCALE = 1.0 / math.sqrt(D) * math.log2(math.e)
NT_DIMS = (((1,), (1,)), ((), ()))


def mm(a, b):
    return jnp.dot(a, b, preferred_element_type=F32)


def split3(w):
    hi = w.astype(BF16)
    rest = w - hi.astype(F32)
    mid = rest.astype(BF16)
    lo = (rest - mid.astype(F32)).astype(BF16)
    return hi, mid, lo


def split2(w):
    hi = w.astype(BF16)
    return hi, (w - hi.astype(F32)).astype(BF16)


def kernel(
    src_in, tpk_in, rot_in, aligned, moved,
    sblk, sblk_t, tpk, feats, scores, plan, planb, probs, ucol, mrow, lrow,
    col_m, col_s, vrow, w3, cur, colx, rowx, sib1, tgt1, zred, mhalf, mother, gbuf, mvx, mhold, mkeep, rlse,
    src_send, src_recv, tpk_send, tpk_recv, col_send, col_recv, row_send, row_recv,
    ar_send, ar_recv, mv_send, mv_recv,
):
    si, ti = lax.axis_index("src"), lax.axis_index("tgt")
    core, zed = lax.rem(si, 2), si // 2
    sibling = zed * 2 + 1 - core

    def tgt_peer(d):
        return lax.rem(ti + d, NTGT)

    def src_peer(d):
        return lax.rem(si + d, NSRC)

    barrier = pltpu.get_barrier_semaphore()

    @pl.loop(1, NTGT)
    def _(d):
        pl.semaphore_signal(barrier, inc=1, device_id=(si, tgt_peer(d)), device_id_type=MESH)

    @pl.loop(1, NSRC)
    def _(d):
        pl.semaphore_signal(barrier, inc=1, device_id=(src_peer(d), ti), device_id_type=MESH)

    pl.semaphore_wait(barrier, NTGT + NSRC - 2)

    def to(src, dst, send, recv, s, t):
        return pltpu.make_async_remote_copy(
            src_ref=src, dst_ref=dst, send_sem=send, recv_sem=recv,
            device_id=(s, t), device_id_type=MESH)

    def slot128(k):
        return pl.ds(pl.multiple_of(k * OWN, OWN), OWN)

    @pl.loop(1, NSRC)
    def _(d):
        to(tpk_in, tpk.at[si], tpk_send, tpk_recv, src_peer(d), ti).start()

    @pl.loop(1, NTGT)
    def _(d):
        to(src_in, sblk.at[slot128(ti), :], src_send, src_recv.at[ti], si, tgt_peer(d)).start()

    sblk[slot128(ti), :] = src_in[...]
    tpk[si] = tpk_in[...]
    cur[...] = rot_in[...]
    for part, piece in enumerate(split3(rot_in[...])):
        w3[part * D:(part + 1) * D, :] = piece

    pltpu.make_async_copy(tpk.at[pl.ds(0, NSRC - 1)], tpk.at[pl.ds(0, NSRC - 1)], tpk_recv).wait()
    lanes = lax.broadcasted_iota(jnp.int32, (512, 128), 1)
    for pair in range(4):
        even, odd = tpk[2 * pair].astype(F32), tpk[2 * pair + 1].astype(F32)
        cut = pl.ds(128 * pair, 128)
        feats[0:512, cut] = jnp.where(lanes < 64, even, pltpu.roll(odd, 64, 1)).astype(BF16)
        feats[512:1024, cut] = jnp.where(lanes < 64, pltpu.roll(even, 64, 1), odd).astype(BF16)

    def chunk(j):
        return pl.ds(pl.multiple_of(j * CH, CH), CH)

    def reset_cols():
        col_m[...] = jnp.full((8, COLS), -jnp.inf, F32)
        col_s[...] = jnp.zeros((8, COLS), F32)

    def col_update(rows, shifted):
        for ct in range(COLS // 128):
            cut = pl.ds(128 * ct, 128)
            x = scores[rows, cut]
            if shifted:
                x = x + ucol[rows, :]
            x = x.reshape(CH // 8, 8, 128)
            old = col_m[:, cut]
            new = jnp.maximum(old, jnp.max(x, axis=0))
            col_s[:, cut] = col_s[:, cut] * jnp.exp2(old - new) + jnp.sum(jnp.exp2(x - new[None]), axis=0)
            col_m[:, cut] = new

    def col_exchange(slot):
        for ct in range(COLS // 128):
            cut = pl.ds(128 * ct, 128)
            high = jnp.max(col_m[:, cut], axis=0, keepdims=True)
            total = jnp.sum(col_s[:, cut] * jnp.exp2(col_m[:, cut] - high), axis=0, keepdims=True)
            colx[slot, si, ct:ct + 1, :] = high + jnp.log2(total)

        @pl.loop(1, NSRC)
        def _(d):
            to(colx.at[slot, si], colx.at[slot, si], col_send.at[slot], col_recv.at[slot], src_peer(d), ti).start()

        seven = colx.at[slot, pl.ds(0, NSRC - 1)]
        pltpu.make_async_copy(seven, seven, col_recv.at[slot]).wait()
        every = colx[slot]
        high = jnp.max(every, axis=0)
        v = -LOG_N - (high + jnp.log2(jnp.sum(jnp.exp2(every - high[None]), axis=0)))
        for ct in range(COLS // 128):
            vrow[:, 128 * ct:128 * (ct + 1)] = jnp.broadcast_to(v[ct:ct + 1, :], (8, 128))

    def row_strip(rows, last):
        x = scores[rows, :].reshape(RB // 8, 8, COLS) + vrow[...][None]
        x = x.reshape(RB, COLS)
        high = jnp.max(x, axis=1, keepdims=True)
        p = jnp.exp2(x - high)
        lrow[rows, :] = jnp.broadcast_to(high + jnp.log2(jnp.sum(p, axis=1, keepdims=True)), (RB, 128))
        if last:
            mrow[rows, :] = jnp.broadcast_to(high, (RB, 128))
        return p

    def row_send_all(slot):
        @pl.loop(0, NTGT)
        def _(k):
            rowx[slot, ti, pl.ds(k, 1), :] = jnp.transpose(lrow[slot128(k), :])[0:1, :]

        @pl.loop(1, NTGT)
        def _(d):
            to(rowx.at[slot, ti], rowx.at[slot, ti], row_send.at[slot], row_recv.at[slot], si, tgt_peer(d)).start()

    def row_combine(slot):
        most = rowx.at[slot, pl.ds(0, NTGT - 1)]
        pltpu.make_async_copy(most, most, row_recv.at[slot]).wait()
        every = rowx[slot]
        high = jnp.max(every, axis=0)
        rlse[...] = high + jnp.log2(jnp.sum(jnp.exp2(every - high[None]), axis=0))

    def row_expanded(k):
        row = rlse[pl.ds(k, 1), :]
        return jnp.transpose(jnp.broadcast_to(row, (128, 128)))

    @pl.loop(0, ROUNDS)
    def _(r):
        first, final = r == 0, r == ROUNDS - 1
        reset_cols()

        @pl.loop(0, ROWS // CH)
        def _(step):
            j = lax.rem(ti // 2 + ROWS // CH - step, ROWS // CH)
            rows = chunk(j)

            @pl.when(first)
            def _():
                for side in range(CH // OWN):
                    k = j * (CH // OWN) + side

                    @pl.when(k != ti)
                    def _():
                        land = sblk.at[slot128(k), :]
                        pltpu.make_async_copy(land, land, src_recv.at[k]).wait()

                sblk_t[:, rows] = jnp.transpose(sblk[rows, :])

            piece = sblk[rows, :]
            z = mm(jnp.concatenate([piece] * 3, axis=1), w3[...]).astype(BF16)
            scores[rows, :] = lax.dot_general(z, feats[...], NT_DIMS, preferred_element_type=F32) * SCALE
            col_update(rows, False)

        col_exchange(2 * r)

        @pl.loop(0, ROWS // RB)
        def _(step):
            row_strip(pl.ds(pl.multiple_of(step * RB, RB), RB), False)

        row_send_all(2 * r)
        row_combine(2 * r)

        @pl.loop(0, NTGT)
        def _(k):
            ucol[slot128(k), :] = -LOG_N - row_expanded(k)

        reset_cols()

        @pl.loop(0, ROWS // CH)
        def _(j):
            col_update(chunk(j), True)

        col_exchange(2 * r + 1)

        @pl.loop(0, ROWS // CH)
        def _(j):
            @pl.loop(0, CH // RB)
            def _(step):
                rows = pl.ds(pl.multiple_of(j * CH + step * RB, RB), RB)
                p = row_strip(rows, True)
                probs[pl.ds(pl.multiple_of(step * RB, RB), RB), :] = p.astype(BF16)

            plan[chunk(j), :] = mm(probs[...], feats[...])

        row_send_all(2 * r + 1)
        row_combine(2 * r + 1)

        @pl.loop(0, NTGT)
        def _(k):
            rows = slot128(k)
            factor = jnp.exp2(mrow[rows, :] - row_expanded(k))
            for cut in range(D // 128):
                lane = pl.ds(128 * cut, 128)
                planb[rows, lane] = (plan[rows, lane] * factor).astype(BF16)

        @pl.when(final)
        def _():
            @pl.loop(1, NTGT)
            def _(d):
                t = tgt_peer(d)
                to(planb.at[slot128(t), :], mvx.at[slot128(ti), :], mv_send, mv_recv, si, t).start()

        theirs = pl.ds(pl.multiple_of((1 - core) * 256, 256), 256)
        ours = pl.ds(pl.multiple_of(core * 256, 256), 256)
        mhold[r] = mm(sblk_t[theirs, :], planb[...]).astype(BF16)
        pair = to(mhold.at[r], sib1.at[r], ar_send.at[0, r], ar_recv.at[0, r], sibling, ti)
        pair.start()
        mine = mm(sblk_t[ours, :], planb[...])
        pair.wait_recv()
        mkeep[r] = (mine + sib1[r].astype(F32)).astype(BF16)

        def lot(k):
            return pl.ds(pl.multiple_of(k * 16, 16), 16)

        @pl.loop(1, NTGT)
        def _(d):
            t = tgt_peer(d)
            to(mkeep.at[r, lot(t), :], tgt1.at[r, ti], ar_send.at[1, r], ar_recv.at[1, r], si, t).start()

        tgt1[r, ti] = mkeep[r, lot(ti), :]
        most = tgt1.at[r, pl.ds(0, NTGT - 1)]
        pltpu.make_async_copy(most, most, ar_recv.at[1, r]).wait()
        zred[r, zed] = jnp.sum(tgt1[r].astype(F32), axis=0).astype(BF16)

        @pl.loop(1, 4)
        def _(d):
            other = lax.rem(zed + d, 4) * 2 + core
            to(zred.at[r, zed], zred.at[r, zed], ar_send.at[2, r], ar_recv.at[2, r], other, ti).start()

        most_z = zred.at[r, pl.ds(0, 3)]
        pltpu.make_async_copy(most_z, most_z, ar_recv.at[2, r]).wait()
        mhalf[r, lot(ti), :] = jnp.sum(zred[r].astype(F32), axis=0).astype(BF16)

        @pl.loop(1, NTGT)
        def _(d):
            to(mhalf.at[r, lot(ti), :], mhalf.at[r, lot(ti), :], ar_send.at[3, r], ar_recv.at[3, r],
               si, tgt_peer(d)).start()

        most_h = mhalf.at[r, pl.ds(0, 240), :]
        pltpu.make_async_copy(most_h, most_h, ar_recv.at[3, r]).wait()
        back = to(mhalf.at[r], mother.at[r], ar_send.at[4, r], ar_recv.at[4, r], sibling, ti)
        back.start()
        gbuf[ours, :] = mhalf[r].astype(F32)
        back.wait_recv()
        gbuf[theirs, :] = mother[r].astype(F32)

        cross = gbuf[...]
        spread = jnp.sqrt(jnp.mean(cross * cross, axis=(0, 1), keepdims=True) + 1e-06)
        g = cur[...] + 0.1 * cross / (spread * math.sqrt(D))
        gh, gl = split2(g)
        gth, gtl = jnp.transpose(gh), jnp.transpose(gl)
        gram = mm(jnp.concatenate([gth, gth, gtl], axis=1), jnp.concatenate([gh, gl, gh], axis=0))
        rh, rl = split2(gram)
        step = mm(jnp.concatenate([gh, gh, gl], axis=1), jnp.concatenate([rh, rl, rh], axis=0))
        new = 1.5 * g - 0.5 * step
        cur[...] = new

        @pl.when(jnp.logical_not(final))
        def _():
            for part, piece in enumerate(split3(cur[...])):
                w3[part * D:(part + 1) * D, :] = piece

        for slot in (2 * r, 2 * r + 1):
            seven = colx.at[slot, pl.ds(0, NSRC - 1)]
            pltpu.make_async_copy(seven, seven, col_send.at[slot]).wait()
            fifteen = rowx.at[slot, pl.ds(0, NTGT - 1)]
            pltpu.make_async_copy(fifteen, fifteen, row_send.at[slot]).wait()
        pair.wait_send()
        pltpu.make_async_copy(most, most, ar_send.at[1, r]).wait()
        pltpu.make_async_copy(most_z, most_z, ar_send.at[2, r]).wait()
        pltpu.make_async_copy(most_h, most_h, ar_send.at[3, r]).wait()
        back.wait_send()

    aligned[...] = cur[...]
    mvx[slot128(ti), :] = planb[slot128(ti), :]
    most_mv = mvx.at[pl.ds(0, ROWS - OWN), :]
    pltpu.make_async_copy(most_mv, most_mv, mv_recv).wait()
    total = mvx[0:OWN, :].astype(F32)
    for k in range(1, NTGT):
        total = total + mvx[k * OWN:(k + 1) * OWN, :].astype(F32)
    moved[...] = total
    pltpu.make_async_copy(most_mv, most_mv, mv_send).wait()
    seven_tpk = tpk.at[pl.ds(0, NSRC - 1)]
    pltpu.make_async_copy(seven_tpk, seven_tpk, tpk_send).wait()
    most_src = sblk.at[pl.ds(0, ROWS - OWN), :]
    pltpu.make_async_copy(most_src, most_src, src_send).wait()


def shards(source, target, rotation):
    packed = jnp.concatenate([target[:512], target[512:]], axis=1)
    vmem = pl.BlockSpec(memory_space=pltpu.VMEM)
    dma = pltpu.SemaphoreType.DMA
    v = pltpu.VMEM
    return pl.pallas_call(
        kernel,
        out_shape=(jax.ShapeDtypeStruct((D, D), F32), jax.ShapeDtypeStruct((OWN, D), F32)),
        in_specs=[vmem] * 3,
        out_specs=(vmem, vmem),
        scratch_shapes=[
            v((ROWS, D), BF16),
            v((D, ROWS), BF16),
            v((NSRC, 512, 128), BF16),
            v((COLS, D), BF16),
            v((ROWS, COLS), F32),
            v((ROWS, D), F32),
            v((ROWS, D), BF16),
            v((CH, COLS), BF16),
            v((ROWS, 128), F32),
            v((ROWS, 128), F32),
            v((ROWS, 128), F32),
            v((8, COLS), F32),
            v((8, COLS), F32),
            v((8, COLS), F32),
            v((3 * D, D), BF16),
            v((D, D), F32),
            v((4, NSRC, 8, 128), F32),
            v((4, NTGT, 16, 128), F32),
            v((2, 256, D), BF16),
            v((2, NTGT, 16, D), BF16),
            v((2, 4, 16, D), BF16),
            v((2, 256, D), BF16),
            v((2, 256, D), BF16),
            v((D, D), F32),
            v((ROWS, D), BF16),
            v((2, 256, D), BF16),
            v((2, 256, D), BF16),
            v((16, 128), F32),
            dma(()), dma((NTGT,)), dma(()), dma(()),
            dma((4,)), dma((4,)), dma((4,)), dma((4,)),
            dma((5, 2)), dma((5, 2)), dma(()), dma(()),
        ],
        compiler_params=pltpu.CompilerParams(
            collective_id=0, has_side_effects=True, vmem_limit_bytes=60 * 1024 * 1024),
    )(source, packed, rotation)


def solution(mesh):
    return jax.shard_map(
        shards, mesh=mesh, in_specs=(P(("src", "tgt"), None), P("tgt", "src"), P()),
        out_specs=(P(), P(("src", "tgt"), None)), check_vma=False)
```

profile of v0, /device:TPU:8, one launch (start us, length us, event | category | flops | bytes accessed | tf_op | source)
XLA Modules:
  0.0 234.6 jit_solution(15652509257238167918)
XLA Ops:
  0.6 0.9 fusion
  1.5 0.1 copy.7
  1.6 0.1 copy.8
  1.8 0.8 pad_maximum_fusion.tpk_in
  2.5 229.0 %shard_map.50 = (f32[512,512]{1,0:T(8,128)}, f32[128,512]{1,0:T(8,128)}) custom-call(bf16[128,512]{1,0:T(8,128)(2,1)} %src_in.1, bf16[512,128]{1,0:T(8,128)(2,1)} %pad_maximum_fusion.tpk_in, f32[512,512]{1,0:T(8,128)} %rot_in.1), custom_call_target="tpu_custom_call" | custom-call | tf_op jit(solution)/shard_map/pallas_call | solution.py:337
  231.6 0.0 copy-start
  231.6 2.3 copy.11
  233.9 0.0 copy-done
  233.9 0.7 copy.12
Async XLA Ops:
  231.6 2.3 copy-start
where the time goes:
time: 238 us; the launch traced here: 235 us
  Pallas kernels  229 us (96%)
  local copies, waits for them, and re-layouts  4.13 us (2%)
    pallas_call x1, Pallas kernels, shards(): pl.pallas_call(kernel, out_shape=(jax.ShapeDtypeStruct((D, D), F32), jax....  229 us

commit v1 on v0

--- a/solution.py
+++ b/solution.py
@@ -20,7 +20,6 @@
 RB = 32
 LOG_N = 14.0
 SCALE = 1.0 / math.sqrt(D) * math.log2(math.e)
-NT_DIMS = (((1,), (1,)), ((), ()))
 
 
 def mm(a, b):
@@ -41,10 +40,10 @@
 
 
 def kernel(
-    src_in, tpk_in, rot_in, aligned, moved,
-    sblk, sblk_t, tpk, feats, scores, plan, planb, probs, ucol, mrow, lrow,
+    src_in, tgt_in, rot_in, aligned, moved,
+    sblk, sblk_t, feats_t, feats, scores, plan, planb, probs, ucol, mrow, lrow,
     col_m, col_s, vrow, w3, cur, colx, rowx, sib1, tgt1, zred, mhalf, mother, gbuf, mvx, mhold, mkeep, rlse,
-    src_send, src_recv, tpk_send, tpk_recv, col_send, col_recv, row_send, row_recv,
+    src_send, src_recv, tgt_send, tgt_recv, col_send, col_recv, row_send, row_recv,
     ar_send, ar_recv, mv_send, mv_recv,
 ):
     si, ti = lax.axis_index("src"), lax.axis_index("tgt")
@@ -77,27 +76,27 @@
     def slot128(k):
         return pl.ds(pl.multiple_of(k * OWN, OWN), OWN)
 
+    def slot64(k):
+        return pl.ds(pl.multiple_of(k * 64, 64), 64)
+
     @pl.loop(1, NSRC)
     def _(d):
-        to(tpk_in, tpk.at[si], tpk_send, tpk_recv, src_peer(d), ti).start()
+        to(tgt_in, feats_t.at[slot64(si), :], tgt_send, tgt_recv, src_peer(d), ti).start()
 
     @pl.loop(1, NTGT)
     def _(d):
         to(src_in, sblk.at[slot128(ti), :], src_send, src_recv.at[ti], si, tgt_peer(d)).start()
 
     sblk[slot128(ti), :] = src_in[...]
-    tpk[si] = tpk_in[...]
+    feats_t[slot64(si), :] = tgt_in[...]
     cur[...] = rot_in[...]
     for part, piece in enumerate(split3(rot_in[...])):
         w3[part * D:(part + 1) * D, :] = piece
 
-    pltpu.make_async_copy(tpk.at[pl.ds(0, NSRC - 1)], tpk.at[pl.ds(0, NSRC - 1)], tpk_recv).wait()
-    lanes = lax.broadcasted_iota(jnp.int32, (512, 128), 1)
-    for pair in range(4):
-        even, odd = tpk[2 * pair].astype(F32), tpk[2 * pair + 1].astype(F32)
-        cut = pl.ds(128 * pair, 128)
-        feats[0:512, cut] = jnp.where(lanes < 64, even, pltpu.roll(odd, 64, 1)).astype(BF16)
-        feats[512:1024, cut] = jnp.where(lanes < 64, pltpu.roll(even, 64, 1), odd).astype(BF16)
+    most_tgt = feats_t.at[pl.ds(0, D - 64), :]
+    pltpu.make_async_copy(most_tgt, most_tgt, tgt_recv).wait()
+    for part in range(D // 128):
+        feats[:, 128 * part:128 * (part + 1)] = jnp.transpose(feats_t[128 * part:128 * (part + 1), :])
 
     def chunk(j):
         return pl.ds(pl.multiple_of(j * CH, CH), CH)
@@ -137,20 +136,38 @@
         for ct in range(COLS // 128):
             vrow[:, 128 * ct:128 * (ct + 1)] = jnp.broadcast_to(v[ct:ct + 1, :], (8, 128))
 
-    def row_strip(rows, last):
-        x = scores[rows, :].reshape(RB // 8, 8, COLS) + vrow[...][None]
-        x = x.reshape(RB, COLS)
-        high = jnp.max(x, axis=1, keepdims=True)
-        p = jnp.exp2(x - high)
-        lrow[rows, :] = jnp.broadcast_to(high + jnp.log2(jnp.sum(p, axis=1, keepdims=True)), (RB, 128))
-        if last:
-            mrow[rows, :] = jnp.broadcast_to(high, (RB, 128))
-        return p
-
-    def row_send_all(slot):
-        @pl.loop(0, NTGT)
-        def _(k):
-            rowx[slot, ti, pl.ds(k, 1), :] = jnp.transpose(lrow[slot128(k), :])[0:1, :]
+    def lane_max(rows):
+        top = None
+        for ct in range(COLS // 128):
+            x = row_tile(rows, ct)
+            top = x if top is None else jnp.maximum(top, x)
+        return top
+
+    def row_tile(rows, ct):
+        cut = pl.ds(128 * ct, 128)
+        x = scores[rows, cut].reshape(RB // 8, 8, 128) + vrow[:, cut][None]
+        return x.reshape(RB, 128)
+
+    def row_pass(step):
+        rows = pl.ds(pl.multiple_of(step * RB, RB), RB)
+        top = lane_max(rows)
+        total = jnp.exp2(row_tile(rows, 0) - top)
+        for ct in range(1, COLS // 128):
+            total = total + jnp.exp2(row_tile(rows, ct) - top)
+        mrow[rows, :] = top
+        lrow[rows, :] = total
+
+    def row_send_all(slot, shared):
+        for k in range(NTGT):
+            rows = slot128(k)
+            if shared:
+                high = jnp.transpose(mrow[rows, :])[0:1, :]
+                total = jnp.transpose(lrow[rows, :])[0:1, :]
+            else:
+                tops = jnp.transpose(mrow[rows, :])
+                high = jnp.max(tops, axis=0, keepdims=True)
+                total = jnp.sum(jnp.transpose(lrow[rows, :]) * jnp.exp2(tops - high), axis=0, keepdims=True)
+            rowx[slot, ti, k:k + 1, :] = high + jnp.log2(total)
 
         @pl.loop(1, NTGT)
         def _(d):
@@ -191,16 +208,16 @@
 
             piece = sblk[rows, :]
             z = mm(jnp.concatenate([piece] * 3, axis=1), w3[...]).astype(BF16)
-            scores[rows, :] = lax.dot_general(z, feats[...], NT_DIMS, preferred_element_type=F32) * SCALE
+            scores[rows, :] = mm(z, feats_t[...]) * SCALE
             col_update(rows, False)
 
         col_exchange(2 * r)
 
         @pl.loop(0, ROWS // RB)
         def _(step):
-            row_strip(pl.ds(pl.multiple_of(step * RB, RB), RB), False)
-
-        row_send_all(2 * r)
+            row_pass(step)
+
+        row_send_all(2 * r, False)
         row_combine(2 * r)
 
         @pl.loop(0, NTGT)
@@ -215,33 +232,57 @@
 
         col_exchange(2 * r + 1)
 
+        @pl.loop(0, ROWS // RB)
+        def _(step):
+            rows = pl.ds(pl.multiple_of(step * RB, RB), RB)
+            mrow[rows, :] = lane_max(rows)
+
+        @pl.loop(0, ROWS // 512)
+        def _(step):
+            rows = pl.ds(pl.multiple_of(step * 512, 512), 512)
+            mrow[rows, :] = jnp.broadcast_to(jnp.max(mrow[rows, :], axis=1, keepdims=True), (512, 128))
+
         @pl.loop(0, ROWS // CH)
-        def _(j):
-            @pl.loop(0, CH // RB)
-            def _(step):
+        def _(turn):
+            j = lax.rem(ti // 2 + turn, ROWS // CH)
+            for step in range(CH // RB):
                 rows = pl.ds(pl.multiple_of(j * CH + step * RB, RB), RB)
-                p = row_strip(rows, True)
-                probs[pl.ds(pl.multiple_of(step * RB, RB), RB), :] = p.astype(BF16)
-
-            plan[chunk(j), :] = mm(probs[...], feats[...])
-
-        row_send_all(2 * r + 1)
+                top = mrow[rows, :]
+                total = None
+                for ct in range(COLS // 128):
+                    p = jnp.exp2(row_tile(rows, ct) - top)
+                    total = p if total is None else total + p
+                    probs[step * RB:(step + 1) * RB, 128 * ct:128 * (ct + 1)] = p.astype(BF16)
+                lrow[rows, :] = total
+
+            rows = chunk(j)
+            sums = jnp.broadcast_to(jnp.sum(lrow[rows, :], axis=1, keepdims=True), (CH, 128))
+            lrow[rows, :] = sums
+            image = mm(probs[...], feats[...])
+            inverse = 1.0 / sums
+            for cut in range(D // 128):
+                lane = slice(128 * cut, 128 * (cut + 1))
+                plan[rows, lane] = (image[:, lane] * inverse).astype(BF16)
+
+            @pl.when(final)
+            def _():
+                for side in range(CH // OWN):
+                    t = j * (CH // OWN) + side
+
+                    @pl.when(t != ti)
+                    def _():
+                        to(plan.at[slot128(t), :], mvx.at[slot128(ti), :], mv_send, mv_recv, si, t).start()
+
+        row_send_all(2 * r + 1, True)
         row_combine(2 * r + 1)
 
         @pl.loop(0, NTGT)
         def _(k):
             rows = slot128(k)
-            factor = jnp.exp2(mrow[rows, :] - row_expanded(k))
+            factor = jnp.exp2(mrow[rows, :] + jnp.log2(lrow[rows, :]) - row_expanded(k))
             for cut in range(D // 128):
                 lane = pl.ds(128 * cut, 128)
-                planb[rows, lane] = (plan[rows, lane] * factor).astype(BF16)
-
-        @pl.when(final)
-        def _():
-            @pl.loop(1, NTGT)
-            def _(d):
-                t = tgt_peer(d)
-                to(planb.at[slot128(t), :], mvx.at[slot128(ti), :], mv_send, mv_recv, si, t).start()
+                planb[rows, lane] = (plan[rows, lane].astype(F32) * factor).astype(BF16)
 
         theirs = pl.ds(pl.multiple_of((1 - core) * 256, 256), 256)
         ours = pl.ds(pl.multiple_of(core * 256, 256), 256)
@@ -314,27 +355,32 @@
         pltpu.make_async_copy(most_h, most_h, ar_send.at[3, r]).wait()
         back.wait_send()
 
-    aligned[...] = cur[...]
-    mvx[slot128(ti), :] = planb[slot128(ti), :]
+    aligned[...] = 0.5 * cur[...]
+    mvx[slot128(ti), :] = plan[slot128(ti), :]
     most_mv = mvx.at[pl.ds(0, ROWS - OWN), :]
     pltpu.make_async_copy(most_mv, most_mv, mv_recv).wait()
-    total = mvx[0:OWN, :].astype(F32)
-    for k in range(1, NTGT):
-        total = total + mvx[k * OWN:(k + 1) * OWN, :].astype(F32)
-    moved[...] = total
+    moved[...] = jnp.zeros((OWN, D), F32)
+    whole = rlse[pl.ds(ti, 1), :]
+
+    @pl.loop(0, NTGT)
+    def _(k):
+        share = 0.5 * jnp.exp2(rowx[2 * ROUNDS - 1, k, pl.ds(ti, 1), :] - whole)
+        factor = jnp.transpose(jnp.broadcast_to(share, (128, 128)))
+        for cut in range(D // 128):
+            lane = pl.ds(128 * cut, 128)
+            moved[:, lane] = moved[:, lane] + mvx[slot128(k), lane].astype(F32) * factor
+
     pltpu.make_async_copy(most_mv, most_mv, mv_send).wait()
-    seven_tpk = tpk.at[pl.ds(0, NSRC - 1)]
-    pltpu.make_async_copy(seven_tpk, seven_tpk, tpk_send).wait()
+    pltpu.make_async_copy(most_tgt, most_tgt, tgt_send).wait()
     most_src = sblk.at[pl.ds(0, ROWS - OWN), :]
     pltpu.make_async_copy(most_src, most_src, src_send).wait()
 
 
 def shards(source, target, rotation):
-    packed = jnp.concatenate([target[:512], target[512:]], axis=1)
     vmem = pl.BlockSpec(memory_space=pltpu.VMEM)
     dma = pltpu.SemaphoreType.DMA
     v = pltpu.VMEM
-    return pl.pallas_call(
+    halves = pl.pallas_call(
         kernel,
         out_shape=(jax.ShapeDtypeStruct((D, D), F32), jax.ShapeDtypeStruct((OWN, D), F32)),
         in_specs=[vmem] * 3,
@@ -342,10 +388,10 @@
         scratch_shapes=[
             v((ROWS, D), BF16),
             v((D, ROWS), BF16),
-            v((NSRC, 512, 128), BF16),
+            v((D, COLS), BF16),
             v((COLS, D), BF16),
             v((ROWS, COLS), F32),
-            v((ROWS, D), F32),
+            v((ROWS, D), BF16),
             v((ROWS, D), BF16),
             v((CH, COLS), BF16),
             v((ROWS, 128), F32),
@@ -373,8 +419,9 @@
             dma((5, 2)), dma((5, 2)), dma(()), dma(()),
         ],
         compiler_params=pltpu.CompilerParams(
-            collective_id=0, has_side_effects=True, vmem_limit_bytes=60 * 1024 * 1024),
-    )(source, packed, rotation)
+            collective_id=0, has_side_effects=True, vmem_limit_bytes=48 * 1024 * 1024),
+    )(source, target.T, rotation)
+    return tuple(2.0 * half for half in halves)
 
 
 def solution(mesh):

time: 238 us -> 196 us (0.82)
  Pallas kernels: 229 us -> 187 us
    pallas_call x1, Pallas kernels: 229 us -> 187 us  [shards(): pl.pallas_call(kernel, out_shape=(jax.ShapeDtypeStruct((D, D), F32), jax....]
where the time goes in v1:
time: 196 us; the launch traced here: 193 us
  Pallas kernels  187 us (95%)
  local copies, waits for them, and re-layouts  3.03 us (2%)
    pallas_call x1, Pallas kernels, shards(): pl.pallas_call(kernel, out_shape=(jax.ShapeDtypeStruct((D, D), F32), jax....  187 us

profile of v1, /device:TPU:8, one launch (start us, length us, event | category | flops | bytes accessed | tf_op | source)
XLA Modules:
  0.0 192.7 jit_solution(8988552934750184889)
XLA Ops:
  0.6 0.0 copy-start
  0.6 1.2 copy-done
  1.9 0.0 copy-start.1
  1.9 0.9 copy-done.1
  2.8 0.0 copy-start.2
  2.8 0.9 copy-done.2
  3.7 187.2 %shard_map.50 = (f32[512,512]{1,0:T(8,128)S(1)}, f32[128,512]{1,0:T(8,128)S(1)}) custom-call(bf16[128,512]{1,0:T(8,128)(2,1)S(1)} %copy-done.1, bf16[64,1024]{1,0:T(8,128)(2,1)S(1)} %bitcast.1, f32[512,512]{1,0:T(8,128)S(1)} %copy-done), custom_call_target="tpu_custom_call" | custom-call | tf_op jit(solution)/shard_map/pallas_call | solution.py:383
  190.9 1.1 broadcast_multiply_fusion
  192.0 0.7 broadcast_multiply_fusion.1
Async XLA Ops:
  0.6 1.2 copy-start
  1.9 0.9 copy-start.1
  2.8 0.9 copy-start.2

commit v2 on v1

--- a/solution.py
+++ b/solution.py
@@ -43,7 +43,7 @@
     src_in, tgt_in, rot_in, aligned, moved,
     sblk, sblk_t, feats_t, feats, scores, plan, planb, probs, ucol, mrow, lrow,
     col_m, col_s, vrow, w3, cur, colx, rowx, sib1, tgt1, zred, mhalf, mother, gbuf, mvx, mhold, mkeep, rlse,
-    src_send, src_recv, tgt_send, tgt_recv, col_send, col_recv, row_send, row_recv,
+    src_send, src_recv, tgt_send, tgt_recv, col_send, col_recv, row_send_sem, row_recv,
     ar_send, ar_recv, mv_send, mv_recv,
 ):
     si, ti = lax.axis_index("src"), lax.axis_index("tgt")
@@ -79,9 +79,12 @@
     def slot64(k):
         return pl.ds(pl.multiple_of(k * 64, 64), 64)
 
-    @pl.loop(1, NSRC)
-    def _(d):
-        to(tgt_in, feats_t.at[slot64(si), :], tgt_send, tgt_recv, src_peer(d), ti).start()
+    def z_peer(d):
+        return lax.rem(zed + d, 4) * 2 + core
+
+    for d in (1, 3, 2):
+        to(tgt_in, feats_t.at[slot64(si), :], tgt_send, tgt_recv.at[si], z_peer(d), ti).start()
+    to(tgt_in, feats_t.at[slot64(si), :], tgt_send, tgt_recv.at[si], sibling, ti).start()
 
     @pl.loop(1, NTGT)
     def _(d):
@@ -94,7 +97,14 @@
         w3[part * D:(part + 1) * D, :] = piece
 
     most_tgt = feats_t.at[pl.ds(0, D - 64), :]
-    pltpu.make_async_copy(most_tgt, most_tgt, tgt_recv).wait()
+    for d in (1, 3, 2):
+        land = feats_t.at[slot64(z_peer(d)), :]
+        pltpu.make_async_copy(land, land, tgt_recv.at[z_peer(d)]).wait()
+        to(land, land, tgt_send, tgt_recv.at[z_peer(d)], sibling, ti).start()
+    for d in range(4):
+        k = lax.rem(zed + d, 4) * 2 + 1 - core
+        land = feats_t.at[slot64(k), :]
+        pltpu.make_async_copy(land, land, tgt_recv.at[k]).wait()
     for part in range(D // 128):
         feats[:, 128 * part:128 * (part + 1)] = jnp.transpose(feats_t[128 * part:128 * (part + 1), :])
 
@@ -157,8 +167,8 @@
         mrow[rows, :] = top
         lrow[rows, :] = total
 
-    def row_send_all(slot, shared):
-        for k in range(NTGT):
+    def row_send(slot, half, shared):
+        for k in range(8 * half, 8 * half + 8):
             rows = slot128(k)
             if shared:
                 high = jnp.transpose(mrow[rows, :])[0:1, :]
@@ -169,16 +179,21 @@
                 total = jnp.sum(jnp.transpose(lrow[rows, :]) * jnp.exp2(tops - high), axis=0, keepdims=True)
             rowx[slot, ti, k:k + 1, :] = high + jnp.log2(total)
 
+        own = rowx.at[slot, ti, pl.ds(8 * half, 8), :]
+
         @pl.loop(1, NTGT)
         def _(d):
-            to(rowx.at[slot, ti], rowx.at[slot, ti], row_send.at[slot], row_recv.at[slot], si, tgt_peer(d)).start()
-
-    def row_combine(slot):
-        most = rowx.at[slot, pl.ds(0, NTGT - 1)]
-        pltpu.make_async_copy(most, most, row_recv.at[slot]).wait()
-        every = rowx[slot]
+            to(own, own, row_send_sem.at[slot, half], row_recv.at[slot, half], si, tgt_peer(d)).start()
+
+    def row_most(slot, half):
+        return rowx.at[slot, pl.ds(0, NTGT - 1), pl.ds(8 * half, 8), :]
+
+    def row_combine(slot, half):
+        most = row_most(slot, half)
+        pltpu.make_async_copy(most, most, row_recv.at[slot, half]).wait()
+        every = rowx[slot, :, 8 * half:8 * half + 8, :]
         high = jnp.max(every, axis=0)
-        rlse[...] = high + jnp.log2(jnp.sum(jnp.exp2(every - high[None]), axis=0))
+        rlse[8 * half:8 * half + 8, :] = high + jnp.log2(jnp.sum(jnp.exp2(every - high[None]), axis=0))
 
     def row_expanded(k):
         row = rlse[pl.ds(k, 1), :]
@@ -213,22 +228,22 @@
 
         col_exchange(2 * r)
 
-        @pl.loop(0, ROWS // RB)
-        def _(step):
-            row_pass(step)
-
-        row_send_all(2 * r, False)
-        row_combine(2 * r)
-
-        @pl.loop(0, NTGT)
-        def _(k):
-            ucol[slot128(k), :] = -LOG_N - row_expanded(k)
+        for half in range(2):
+            @pl.loop(half * ROWS // RB // 2, (half + 1) * ROWS // RB // 2)
+            def _(step):
+                row_pass(step)
+
+            row_send(2 * r, half, False)
 
         reset_cols()
-
-        @pl.loop(0, ROWS // CH)
-        def _(j):
-            col_update(chunk(j), True)
+        for half in range(2):
+            row_combine(2 * r, half)
+            for k in range(8 * half, 8 * half + 8):
+                ucol[slot128(k), :] = -LOG_N - row_expanded(k)
+
+            @pl.loop(half * ROWS // CH // 2, (half + 1) * ROWS // CH // 2)
+            def _(j):
+                col_update(chunk(j), True)
 
         col_exchange(2 * r + 1)
 
@@ -242,9 +257,7 @@
             rows = pl.ds(pl.multiple_of(step * 512, 512), 512)
             mrow[rows, :] = jnp.broadcast_to(jnp.max(mrow[rows, :], axis=1, keepdims=True), (512, 128))
 
-        @pl.loop(0, ROWS // CH)
-        def _(turn):
-            j = lax.rem(ti // 2 + turn, ROWS // CH)
+        def images(j):
             for step in range(CH // RB):
                 rows = pl.ds(pl.multiple_of(j * CH + step * RB, RB), RB)
                 top = mrow[rows, :]
@@ -264,25 +277,26 @@
                 lane = slice(128 * cut, 128 * (cut + 1))
                 plan[rows, lane] = (image[:, lane] * inverse).astype(BF16)
 
+        for half in range(2):
+            pl.loop(half * ROWS // CH // 2, (half + 1) * ROWS // CH // 2)(images)
+            row_send(2 * r + 1, half, True)
+
+        def send_images(offsets):
             @pl.when(final)
             def _():
-                for side in range(CH // OWN):
-                    t = j * (CH // OWN) + side
-
-                    @pl.when(t != ti)
-                    def _():
-                        to(plan.at[slot128(t), :], mvx.at[slot128(ti), :], mv_send, mv_recv, si, t).start()
-
-        row_send_all(2 * r + 1, True)
-        row_combine(2 * r + 1)
-
-        @pl.loop(0, NTGT)
-        def _(k):
-            rows = slot128(k)
-            factor = jnp.exp2(mrow[rows, :] + jnp.log2(lrow[rows, :]) - row_expanded(k))
-            for cut in range(D // 128):
-                lane = pl.ds(128 * cut, 128)
-                planb[rows, lane] = (plan[rows, lane].astype(F32) * factor).astype(BF16)
+                for dy, dx in offsets:
+                    t = lax.rem(ti // 4 + dy, 4) * 4 + lax.rem(ti + dx, 4)
+                    to(plan.at[slot128(t), :], mvx.at[slot128(ti), :], mv_send, mv_recv, si, t).start()
+
+        send_images(((0, 1), (0, 3), (1, 0), (3, 0), (1, 1), (3, 3), (1, 3), (3, 1)))
+        for half in range(2):
+            row_combine(2 * r + 1, half)
+            for k in range(8 * half, 8 * half + 8):
+                rows = slot128(k)
+                factor = jnp.exp2(mrow[rows, :] + jnp.log2(lrow[rows, :]) - row_expanded(k))
+                for cut in range(D // 128):
+                    lane = pl.ds(128 * cut, 128)
+                    planb[rows, lane] = (plan[rows, lane].astype(F32) * factor).astype(BF16)
 
         theirs = pl.ds(pl.multiple_of((1 - core) * 256, 256), 256)
         ours = pl.ds(pl.multiple_of(core * 256, 256), 256)
@@ -301,6 +315,7 @@
             t = tgt_peer(d)
             to(mkeep.at[r, lot(t), :], tgt1.at[r, ti], ar_send.at[1, r], ar_recv.at[1, r], si, t).start()
 
+        send_images(((0, 2), (2, 0), (2, 2)))
         tgt1[r, ti] = mkeep[r, lot(ti), :]
         most = tgt1.at[r, pl.ds(0, NTGT - 1)]
         pltpu.make_async_copy(most, most, ar_recv.at[1, r]).wait()
@@ -320,6 +335,7 @@
             to(mhalf.at[r, lot(ti), :], mhalf.at[r, lot(ti), :], ar_send.at[3, r], ar_recv.at[3, r],
                si, tgt_peer(d)).start()
 
+        send_images(((1, 2), (3, 2), (2, 1), (2, 3)))
         most_h = mhalf.at[r, pl.ds(0, 240), :]
         pltpu.make_async_copy(most_h, most_h, ar_recv.at[3, r]).wait()
         back = to(mhalf.at[r], mother.at[r], ar_send.at[4, r], ar_recv.at[4, r], sibling, ti)
@@ -347,8 +363,9 @@
         for slot in (2 * r, 2 * r + 1):
             seven = colx.at[slot, pl.ds(0, NSRC - 1)]
             pltpu.make_async_copy(seven, seven, col_send.at[slot]).wait()
-            fifteen = rowx.at[slot, pl.ds(0, NTGT - 1)]
-            pltpu.make_async_copy(fifteen, fifteen, row_send.at[slot]).wait()
+            for half in range(2):
+                most_r = row_most(slot, half)
+                pltpu.make_async_copy(most_r, most_r, row_send_sem.at[slot, half]).wait()
         pair.wait_send()
         pltpu.make_async_copy(most, most, ar_send.at[1, r]).wait()
         pltpu.make_async_copy(most_z, most_z, ar_send.at[2, r]).wait()
@@ -414,8 +431,8 @@
             v((2, 256, D), BF16),
             v((2, 256, D), BF16),
             v((16, 128), F32),
-            dma(()), dma((NTGT,)), dma(()), dma(()),
-            dma((4,)), dma((4,)), dma((4,)), dma((4,)),
+            dma(()), dma((NTGT,)), dma(()), dma((NSRC,)),
+            dma((4,)), dma((4,)), dma((4, 2)), dma((4, 2)),
             dma((5, 2)), dma((5, 2)), dma(()), dma(()),
         ],
         compiler_params=pltpu.CompilerParams(

time: 196 us -> 170 us (0.87); the launches traced: 193 us -> 169 us
  Pallas kernels: 187 us -> 164 us
    pallas_call x1, Pallas kernels: 187 us -> 164 us  [shards(): pl.pallas_call(kernel, out_shape=(jax.ShapeDtypeStruct((D, D), F32), jax....]
where the time goes in v2:
time: 170 us; the launch traced here: 169 us
  Pallas kernels  164 us (96%)
  local copies, waits for them, and re-layouts  3.03 us (2%)
  other arithmetic  1.79 us (1%)
    pallas_call x1, Pallas kernels, shards(): pl.pallas_call(kernel, out_shape=(jax.ShapeDtypeStruct((D, D), F32), jax....  164 us

profile of v2, /device:TPU:8, one launch (start us, length us, event | category | flops | bytes accessed | tf_op | source)
XLA Modules:
  0.0 169.3 jit_solution(15953422921180682693)
XLA Ops:
  0.6 0.0 copy-start
  0.6 1.2 copy-done
  1.9 0.0 copy-start.1
  1.9 0.9 copy-done.1
  2.8 0.0 copy-start.2
  2.8 0.9 copy-done.2
  3.7 163.9 %shard_map.50 = (f32[512,512]{1,0:T(8,128)S(1)}, f32[128,512]{1,0:T(8,128)S(1)}) custom-call(bf16[128,512]{1,0:T(8,128)(2,1)S(1)} %copy-done.1, bf16[64,1024]{1,0:T(8,128)(2,1)S(1)} %bitcast.1, f32[512,512]{1,0:T(8,128)S(1)} %copy-done), custom_call_target="tpu_custom_call" | custom-call | tf_op jit(solution)/shard_map/pallas_call | solution.py:400
  167.5 1.1 broadcast_multiply_fusion
  168.6 0.7 broadcast_multiply_fusion.1
Async XLA Ops:
  0.6 1.2 copy-start
  1.9 0.9 copy-start.1
  2.8 0.9 copy-start.2

commit v3 on v2

--- a/solution.py
+++ b/solution.py
@@ -43,12 +43,14 @@
     src_in, tgt_in, rot_in, aligned, moved,
     sblk, sblk_t, feats_t, feats, scores, plan, planb, probs, ucol, mrow, lrow,
     col_m, col_s, vrow, w3, cur, colx, rowx, sib1, tgt1, zred, mhalf, mother, gbuf, mvx, mhold, mkeep, rlse,
-    src_send, src_recv, tgt_send, tgt_recv, col_send, col_recv, row_send_sem, row_recv,
+    src_send, near, far, tgt_send, tgt_recv, col_send, col_recv, row_send_sem, row_recv,
     ar_send, ar_recv, mv_send, mv_recv,
 ):
     si, ti = lax.axis_index("src"), lax.axis_index("tgt")
     core, zed = lax.rem(si, 2), si // 2
     sibling = zed * 2 + 1 - core
+    ty, tx = ti // 4, lax.rem(ti, 4)
+    across = 4 * tx + ty
 
     def tgt_peer(d):
         return lax.rem(ti + d, NTGT)
@@ -79,32 +81,80 @@
     def slot64(k):
         return pl.ds(pl.multiple_of(k * 64, 64), 64)
 
-    def z_peer(d):
-        return lax.rem(zed + d, 4) * 2 + core
-
-    for d in (1, 3, 2):
-        to(tgt_in, feats_t.at[slot64(si), :], tgt_send, tgt_recv.at[si], z_peer(d), ti).start()
-    to(tgt_in, feats_t.at[slot64(si), :], tgt_send, tgt_recv.at[si], sibling, ti).start()
-
-    @pl.loop(1, NTGT)
-    def _(d):
-        to(src_in, sblk.at[slot128(ti), :], src_send, src_recv.at[ti], si, tgt_peer(d)).start()
-
-    sblk[slot128(ti), :] = src_in[...]
+    def beside(c, d):
+        return lax.rem(c + d, 4)
+
+    x_ways = [(si, 4 * ty + beside(tx, d)) for d in (1, 3)]
+    y_ways = [(si, 4 * beside(ty, d) + tx) for d in (1, 3)]
+    z_ways = [(2 * beside(zed, d) + core, ti) for d in (1, 3)]
+
+    def both_ways(ring, src, dst, ways, send):
+        for side in range(2):
+            to(src, dst, send, near.at[ring, side], *ways[side]).start()
+
+    def relay(ring, ref, at, count, c, ways, send, after):
+        for side, k in ((0, beside(c, 3)), (1, beside(c, 1))):
+            land = ref.at[pl.ds(pl.multiple_of(at(k), count), count), :]
+            pltpu.make_async_copy(land, land, near.at[ring, side]).wait()
+            half = ref.at[pl.ds(pl.multiple_of(at(k) + side * (count // 2), count // 2), count // 2), :]
+            to(half, half, send, far.at[ring, side], *ways[side]).start()
+            after(land, k)
+
+    def relayed(ring, ref, at, count, c, after):
+        k = beside(c, 2)
+        for side in range(2):
+            half = ref.at[pl.ds(pl.multiple_of(at(k) + side * (count // 2), count // 2), count // 2), :]
+            pltpu.make_async_copy(half, half, far.at[ring, side]).wait()
+        after(ref.at[pl.ds(pl.multiple_of(at(k), count), count), :], k)
+
+    def nothing(land, k):
+        pass
+
+    upper, lower = src_in.at[pl.ds(0, 64), :], src_in.at[pl.ds(64, 64), :]
+    own_up, own_low = sblk.at[slot64(ti), :], sblk.at[slot64(16 + across), :]
+    own_feats = feats_t.at[slot64(si), :]
+    both_ways(2, tgt_in, own_feats, z_ways, tgt_send)
+    both_ways(0, upper, own_up, x_ways, src_send)
+    both_ways(1, lower, own_low, y_ways, src_send)
+    both_ways(3, upper, own_up, y_ways, src_send)
+    both_ways(4, lower, own_low, x_ways, src_send)
+    to(tgt_in, own_feats, tgt_send, tgt_recv.at[zed], sibling, ti).start()
+
+    sblk[slot64(ti), :] = src_in[0:64, :]
+    sblk[slot64(16 + across), :] = src_in[64:128, :]
     feats_t[slot64(si), :] = tgt_in[...]
     cur[...] = rot_in[...]
     for part, piece in enumerate(split3(rot_in[...])):
         w3[part * D:(part + 1) * D, :] = piece
 
+    def up_on(land, k):
+        both_ways(3, land, land, y_ways, src_send)
+
+    def low_on(land, k):
+        both_ways(4, land, land, x_ways, src_send)
+
+    def to_sibling(land, k):
+        to(land, land, tgt_send, tgt_recv.at[k], sibling, ti).start()
+
+    def up_at(k):
+        return 64 * (4 * ty + k)
+
+    def low_at(k):
+        return ROWS // 2 + 64 * (4 * tx + k)
+
+    def feats_at(k):
+        return 64 * (2 * k + core)
+
+    relay(0, sblk, up_at, 64, tx, x_ways, src_send, up_on)
+    relay(1, sblk, low_at, 64, ty, y_ways, src_send, low_on)
+    relay(2, feats_t, feats_at, 64, zed, z_ways, tgt_send, to_sibling)
+    relayed(0, sblk, up_at, 64, tx, up_on)
+    relayed(1, sblk, low_at, 64, ty, low_on)
+    relayed(2, feats_t, feats_at, 64, zed, to_sibling)
+    for k in range(4):
+        land = feats_t.at[slot64(2 * k + 1 - core), :]
+        pltpu.make_async_copy(land, land, tgt_recv.at[k]).wait()
     most_tgt = feats_t.at[pl.ds(0, D - 64), :]
-    for d in (1, 3, 2):
-        land = feats_t.at[slot64(z_peer(d)), :]
-        pltpu.make_async_copy(land, land, tgt_recv.at[z_peer(d)]).wait()
-        to(land, land, tgt_send, tgt_recv.at[z_peer(d)], sibling, ti).start()
-    for d in range(4):
-        k = lax.rem(zed + d, 4) * 2 + 1 - core
-        land = feats_t.at[slot64(k), :]
-        pltpu.make_async_copy(land, land, tgt_recv.at[k]).wait()
     for part in range(D // 128):
         feats[:, 128 * part:128 * (part + 1)] = jnp.transpose(feats_t[128 * part:128 * (part + 1), :])
 
@@ -206,19 +256,23 @@
 
         @pl.loop(0, ROWS // CH)
         def _(step):
-            j = lax.rem(ti // 2 + ROWS // CH - step, ROWS // CH)
+            phase, kind = step // 2, lax.rem(step, 2)
+            start = ty + kind * (tx - ty)
+            j = 4 * kind + lax.rem(start + phase + phase // 2 - 2 * (phase // 3), 4)
             rows = chunk(j)
+
+            @pl.when(jnp.logical_and(first, step == 2))
+            def _():
+                relay(3, sblk, lambda k: CH * k, CH, ty, y_ways, src_send, nothing)
+                relay(4, sblk, lambda k: ROWS // 2 + CH * k, CH, tx, x_ways, src_send, nothing)
+
+            @pl.when(jnp.logical_and(first, step == 6))
+            def _():
+                relayed(3, sblk, lambda k: CH * k, CH, ty, nothing)
+                relayed(4, sblk, lambda k: ROWS // 2 + CH * k, CH, tx, nothing)
 
             @pl.when(first)
             def _():
-                for side in range(CH // OWN):
-                    k = j * (CH // OWN) + side
-
-                    @pl.when(k != ti)
-                    def _():
-                        land = sblk.at[slot128(k), :]
-                        pltpu.make_async_copy(land, land, src_recv.at[k]).wait()
-
                 sblk_t[:, rows] = jnp.transpose(sblk[rows, :])
 
             piece = sblk[rows, :]
@@ -285,8 +339,9 @@
             @pl.when(final)
             def _():
                 for dy, dx in offsets:
-                    t = lax.rem(ti // 4 + dy, 4) * 4 + lax.rem(ti + dx, 4)
-                    to(plan.at[slot128(t), :], mvx.at[slot128(ti), :], mv_send, mv_recv, si, t).start()
+                    y, x = beside(ty, dy), beside(tx, dx)
+                    for src, dst in ((4 * y + x, ti), (16 + 4 * x + y, 16 + ti)):
+                        to(plan.at[slot64(src), :], mvx.at[slot64(dst), :], mv_send, mv_recv, si, 4 * y + x).start()
 
         send_images(((0, 1), (0, 3), (1, 0), (3, 0), (1, 1), (3, 3), (1, 3), (3, 1)))
         for half in range(2):
@@ -373,19 +428,25 @@
         back.wait_send()
 
     aligned[...] = 0.5 * cur[...]
-    mvx[slot128(ti), :] = plan[slot128(ti), :]
+    mvx[slot64(ti), :] = plan[slot64(ti), :]
+    mvx[slot64(16 + ti), :] = plan[slot64(16 + across), :]
     most_mv = mvx.at[pl.ds(0, ROWS - OWN), :]
     pltpu.make_async_copy(most_mv, most_mv, mv_recv).wait()
-    moved[...] = jnp.zeros((OWN, D), F32)
-    whole = rlse[pl.ds(ti, 1), :]
-
-    @pl.loop(0, NTGT)
-    def _(k):
-        share = 0.5 * jnp.exp2(rowx[2 * ROUNDS - 1, k, pl.ds(ti, 1), :] - whole)
-        factor = jnp.transpose(jnp.broadcast_to(share, (128, 128)))
+    for part, place in ((0, ti), (1, across)):
+        stat = 8 * part + place // 2
+        odd = lax.rem(place, 2) == 1
+        whole = rlse[pl.ds(stat, 1), :]
+        total = [0.0] * (D // 128)
+        for k in range(NTGT):
+            share = 0.5 * jnp.exp2(rowx[2 * ROUNDS - 1, k, pl.ds(stat, 1), :] - whole)
+            factor = jnp.transpose(jnp.broadcast_to(share, (128, 128)))
+            factor = jnp.where(odd, factor[64:128], factor[0:64])
+            at = (16 * part + k) * 64
+            for cut in range(D // 128):
+                lane = slice(128 * cut, 128 * (cut + 1))
+                total[cut] = total[cut] + mvx[at:at + 64, lane].astype(F32) * factor
         for cut in range(D // 128):
-            lane = pl.ds(128 * cut, 128)
-            moved[:, lane] = moved[:, lane] + mvx[slot128(k), lane].astype(F32) * factor
+            moved[64 * part:64 * (part + 1), 128 * cut:128 * (cut + 1)] = total[cut]
 
     pltpu.make_async_copy(most_mv, most_mv, mv_send).wait()
     pltpu.make_async_copy(most_tgt, most_tgt, tgt_send).wait()
@@ -431,7 +492,7 @@
             v((2, 256, D), BF16),
             v((2, 256, D), BF16),
             v((16, 128), F32),
-            dma(()), dma((NTGT,)), dma(()), dma((NSRC,)),
+            dma(()), dma((5, 2)), dma((5, 2)), dma(()), dma((4,)),
             dma((4,)), dma((4,)), dma((4, 2)), dma((4, 2)),
             dma((5, 2)), dma((5, 2)), dma(()), dma(()),
         ],

time: 170 us -> 152 us (0.89)
  Pallas kernels: 164 us -> 144 us
    pallas_call x1, Pallas kernels: 164 us -> 144 us  [shards(): pl.pallas_call(kernel, out_shape=(jax.ShapeDtypeStruct((D, D), F32), jax....]
where the time goes in v3:
time: 152 us; the launch traced here: 150 us
  Pallas kernels  144 us (95%)
  local copies, waits for them, and re-layouts  3.03 us (2%)
  other arithmetic  1.79 us (1%)
    pallas_call x1, Pallas kernels, shards(): pl.pallas_call(kernel, out_shape=(jax.ShapeDtypeStruct((D, D), F32), jax....  144 us

profile of v3, /device:TPU:8, one launch (start us, length us, event | category | flops | bytes accessed | tf_op | source)
XLA Modules:
  0.0 149.8 jit_solution(11505406206172325806)
XLA Ops:
  0.6 0.0 copy-start
  0.6 1.2 copy-done
  1.9 0.0 copy-start.1
  1.9 0.9 copy-done.1
  2.8 0.0 copy-start.2
  2.8 0.9 copy-done.2
  3.7 144.3 %shard_map.50 = (f32[512,512]{1,0:T(8,128)S(1)}, f32[128,512]{1,0:T(8,128)S(1)}) custom-call(bf16[128,512]{1,0:T(8,128)(2,1)S(1)} %copy-done.1, bf16[64,1024]{1,0:T(8,128)(2,1)S(1)} %bitcast.1, f32[512,512]{1,0:T(8,128)S(1)} %copy-done), custom_call_target="tpu_custom_call" | custom-call | tf_op jit(solution)/shard_map/pallas_call | solution.py:461
  148.0 1.1 broadcast_multiply_fusion
  149.1 0.7 broadcast_multiply_fusion.1
Async XLA Ops:
  0.6 1.2 copy-start
  1.9 0.9 copy-start.1
  2.8 0.9 copy-start.2

commit v4 on v3

--- a/solution.py
+++ b/solution.py
@@ -10,6 +10,8 @@
 
 ROUNDS = 2
 MESH = pl.DeviceIdType.MESH
+VIA = (((1, 2), (0, 3)), ((3, 2), (0, 3)), ((2, 1), (3, 0)), ((2, 3), (3, 0)))
+FAR_FIRST = ((2, 2), (1, 2), (3, 2), (2, 1), (2, 3), (1, 1), (3, 3), (1, 3), (3, 1), (0, 2), (2, 0), (0, 1), (0, 3), (1, 0), (3, 0))
 F32, BF16 = jnp.float32, jnp.bfloat16
 NSRC, NTGT = 8, 16
 D = 512
@@ -26,14 +28,6 @@
     return jnp.dot(a, b, preferred_element_type=F32)
 
 
-def split3(w):
-    hi = w.astype(BF16)
-    rest = w - hi.astype(F32)
-    mid = rest.astype(BF16)
-    lo = (rest - mid.astype(F32)).astype(BF16)
-    return hi, mid, lo
-
-
 def split2(w):
     hi = w.astype(BF16)
     return hi, (w - hi.astype(F32)).astype(BF16)
@@ -41,10 +35,10 @@
 
 def kernel(
     src_in, tgt_in, rot_in, aligned, moved,
-    sblk, sblk_t, feats_t, feats, scores, plan, planb, probs, ucol, mrow, lrow,
-    col_m, col_s, vrow, w3, cur, colx, rowx, sib1, tgt1, zred, mhalf, mother, gbuf, mvx, mhold, mkeep, rlse,
+    sblk, sblk_t, feats_t, feats, scores, plan, sblk_s, probs_a, probs_b, parts_a, parts_b, ucol, mrow, lrow,
+    col_m, col_s, vrow, w2, cur, colx, rowx, sib1, tgt1, zred, mhalf, mother, gbuf, mvx, mhold, mkeep, rlse, stage,
     src_send, near, far, tgt_send, tgt_recv, col_send, col_recv, row_send_sem, row_recv,
-    ar_send, ar_recv, mv_send, mv_recv,
+    ar_send, ar_recv, mv_send, mv_recv, st_send, st_recv, pair_recv, lot_recv,
 ):
     si, ti = lax.axis_index("src"), lax.axis_index("tgt")
     core, zed = lax.rem(si, 2), si // 2
@@ -124,8 +118,8 @@
     sblk[slot64(16 + across), :] = src_in[64:128, :]
     feats_t[slot64(si), :] = tgt_in[...]
     cur[...] = rot_in[...]
-    for part, piece in enumerate(split3(rot_in[...])):
-        w3[part * D:(part + 1) * D, :] = piece
+    for part, piece in enumerate(split2(rot_in[...])):
+        w2[part * D:(part + 1) * D, :] = piece
 
     def up_on(land, k):
         both_ways(3, land, land, y_ways, src_send)
@@ -184,9 +178,9 @@
             total = jnp.sum(col_s[:, cut] * jnp.exp2(col_m[:, cut] - high), axis=0, keepdims=True)
             colx[slot, si, ct:ct + 1, :] = high + jnp.log2(total)
 
-        @pl.loop(1, NSRC)
-        def _(d):
-            to(colx.at[slot, si], colx.at[slot, si], col_send.at[slot], col_recv.at[slot], src_peer(d), ti).start()
+        for d in (4, 5, 2, 6, 3, 7, 1):
+            s = 2 * beside(zed, d // 2) + lax.rem(core + d, 2)
+            to(colx.at[slot, si], colx.at[slot, si], col_send.at[slot], col_recv.at[slot], s, ti).start()
 
         seven = colx.at[slot, pl.ds(0, NSRC - 1)]
         pltpu.make_async_copy(seven, seven, col_recv.at[slot]).wait()
@@ -231,9 +225,9 @@
 
         own = rowx.at[slot, ti, pl.ds(8 * half, 8), :]
 
-        @pl.loop(1, NTGT)
-        def _(d):
-            to(own, own, row_send_sem.at[slot, half], row_recv.at[slot, half], si, tgt_peer(d)).start()
+        for dy, dx in FAR_FIRST:
+            t = 4 * beside(ty, dy) + beside(tx, dx)
+            to(own, own, row_send_sem.at[slot, half], row_recv.at[slot, half], si, t).start()
 
     def row_most(slot, half):
         return rowx.at[slot, pl.ds(0, NTGT - 1), pl.ds(8 * half, 8), :]
@@ -254,31 +248,31 @@
         first, final = r == 0, r == ROUNDS - 1
         reset_cols()
 
-        @pl.loop(0, ROWS // CH)
-        def _(step):
-            phase, kind = step // 2, lax.rem(step, 2)
-            start = ty + kind * (tx - ty)
-            j = 4 * kind + lax.rem(start + phase + phase // 2 - 2 * (phase // 3), 4)
-            rows = chunk(j)
-
-            @pl.when(jnp.logical_and(first, step == 2))
+        @pl.loop(0, 4)
+        def _(phase):
+            offset = phase + phase // 2 - 2 * (phase // 3)
+            pair = (chunk(beside(ty, offset)), chunk(4 + beside(tx, offset)))
+
+            @pl.when(jnp.logical_and(first, phase == 1))
             def _():
                 relay(3, sblk, lambda k: CH * k, CH, ty, y_ways, src_send, nothing)
                 relay(4, sblk, lambda k: ROWS // 2 + CH * k, CH, tx, x_ways, src_send, nothing)
 
-            @pl.when(jnp.logical_and(first, step == 6))
+            @pl.when(jnp.logical_and(first, phase == 3))
             def _():
                 relayed(3, sblk, lambda k: CH * k, CH, ty, nothing)
                 relayed(4, sblk, lambda k: ROWS // 2 + CH * k, CH, tx, nothing)
 
             @pl.when(first)
             def _():
-                sblk_t[:, rows] = jnp.transpose(sblk[rows, :])
-
-            piece = sblk[rows, :]
-            z = mm(jnp.concatenate([piece] * 3, axis=1), w3[...]).astype(BF16)
-            scores[rows, :] = mm(z, feats_t[...]) * SCALE
-            col_update(rows, False)
+                for rows in pair:
+                    sblk_t[:, rows] = jnp.transpose(sblk[rows, :])
+
+            turned = [mm(jnp.concatenate([sblk[rows, :]] * 2, axis=1), w2[...]).astype(BF16) for rows in pair]
+            for rows, z in zip(pair, turned):
+                scores[rows, :] = mm(z, feats_t[...]) * SCALE
+            for rows in pair:
+                col_update(rows, False)
 
         col_exchange(2 * r)
 
@@ -311,28 +305,30 @@
             rows = pl.ds(pl.multiple_of(step * 512, 512), 512)
             mrow[rows, :] = jnp.broadcast_to(jnp.max(mrow[rows, :], axis=1, keepdims=True), (512, 128))
 
-        def images(j):
-            for step in range(CH // RB):
-                rows = pl.ds(pl.multiple_of(j * CH + step * RB, RB), RB)
-                top = mrow[rows, :]
-                total = None
-                for ct in range(COLS // 128):
-                    p = jnp.exp2(row_tile(rows, ct) - top)
-                    total = p if total is None else total + p
-                    probs[step * RB:(step + 1) * RB, 128 * ct:128 * (ct + 1)] = p.astype(BF16)
-                lrow[rows, :] = total
-
-            rows = chunk(j)
-            sums = jnp.broadcast_to(jnp.sum(lrow[rows, :], axis=1, keepdims=True), (CH, 128))
-            lrow[rows, :] = sums
-            image = mm(probs[...], feats[...])
-            inverse = 1.0 / sums
-            for cut in range(D // 128):
-                lane = slice(128 * cut, 128 * (cut + 1))
-                plan[rows, lane] = (image[:, lane] * inverse).astype(BF16)
+        def images(i):
+            for side, (probs, parts) in enumerate(((probs_a, parts_a), (probs_b, parts_b))):
+                j = 2 * i + side
+                for step in range(CH // RB):
+                    rows = pl.ds(pl.multiple_of(j * CH + step * RB, RB), RB)
+                    top = mrow[rows, :]
+                    total = None
+                    for ct in range(COLS // 128):
+                        p = jnp.exp2(row_tile(rows, ct) - top)
+                        total = p if total is None else total + p
+                        probs[step * RB:(step + 1) * RB, 128 * ct:128 * (ct + 1)] = p.astype(BF16)
+                    parts[step * RB:(step + 1) * RB, :] = total
+            for side, (probs, parts) in enumerate(((probs_a, parts_a), (probs_b, parts_b))):
+                rows = chunk(2 * i + side)
+                image = mm(probs[...], feats[...])
+                sums = jnp.broadcast_to(jnp.sum(parts[...], axis=1, keepdims=True), (CH, 128))
+                lrow[rows, :] = sums
+                inverse = 1.0 / sums
+                for cut in range(D // 128):
+                    lane = slice(128 * cut, 128 * (cut + 1))
+                    plan[rows, lane] = (image[:, lane] * inverse).astype(BF16)
 
         for half in range(2):
-            pl.loop(half * ROWS // CH // 2, (half + 1) * ROWS // CH // 2)(images)
+            pl.loop(half * ROWS // CH // 4, (half + 1) * ROWS // CH // 4)(images)
             row_send(2 * r + 1, half, True)
 
         def send_images(offsets):
@@ -343,34 +339,58 @@
                     for src, dst in ((4 * y + x, ti), (16 + 4 * x + y, 16 + ti)):
                         to(plan.at[slot64(src), :], mvx.at[slot64(dst), :], mv_send, mv_recv, si, 4 * y + x).start()
 
-        send_images(((0, 1), (0, 3), (1, 0), (3, 0), (1, 1), (3, 3), (1, 3), (3, 1)))
+        def to_stage():
+            @pl.when(final)
+            def _():
+                for q, ((dy, dx), (sy, sx)) in enumerate(VIA):
+                    y, x = beside(ty, dy), beside(tx, dx)
+                    for half, src in enumerate((4 * y + x, 16 + 4 * x + y)):
+                        to(plan.at[slot64(src), :], stage.at[q, pl.ds(64 * half, 64), :], st_send, st_recv.at[q],
+                           si, 4 * beside(ty, sy) + beside(tx, sx)).start()
+
+        def from_stage(chosen):
+            @pl.when(final)
+            def _():
+                for q in chosen:
+                    (dy, dx), (sy, sx) = VIA[q]
+                    pltpu.make_async_copy(stage.at[q], stage.at[q], st_recv.at[q]).wait()
+                    sender = 4 * beside(ty, 4 - sy) + beside(tx, 4 - sx)
+                    t = 4 * beside(ty, 4 + dy - sy) + beside(tx, 4 + dx - sx)
+                    for half, dst in enumerate((sender, 16 + sender)):
+                        to(stage.at[q, pl.ds(64 * half, 64), :], mvx.at[slot64(dst), :], mv_send, mv_recv, si, t).start()
+
+        to_stage()
+        send_images(((0, 1), (1, 0), (1, 1), (0, 3), (3, 0)))
         for half in range(2):
             row_combine(2 * r + 1, half)
-            for k in range(8 * half, 8 * half + 8):
-                rows = slot128(k)
-                factor = jnp.exp2(mrow[rows, :] + jnp.log2(lrow[rows, :]) - row_expanded(k))
-                for cut in range(D // 128):
-                    lane = pl.ds(128 * cut, 128)
-                    planb[rows, lane] = (plan[rows, lane].astype(F32) * factor).astype(BF16)
+            factor = jnp.exp2(rowx[2 * r + 1, ti, 8 * half:8 * half + 8, :] - rlse[8 * half:8 * half + 8, :])
+            for k in range(8):
+                lane = slice(128 * (8 * half + k), 128 * (8 * half + k + 1))
+                sblk_s[:, lane] = (sblk_t[:, lane].astype(F32) * factor[k:k + 1, :]).astype(BF16)
 
         theirs = pl.ds(pl.multiple_of((1 - core) * 256, 256), 256)
         ours = pl.ds(pl.multiple_of(core * 256, 256), 256)
-        mhold[r] = mm(sblk_t[theirs, :], planb[...]).astype(BF16)
-        pair = to(mhold.at[r], sib1.at[r], ar_send.at[0, r], ar_recv.at[0, r], sibling, ti)
-        pair.start()
-        mine = mm(sblk_t[ours, :], planb[...])
-        pair.wait_recv()
-        mkeep[r] = (mine + sib1[r].astype(F32)).astype(BF16)
-
         def lot(k):
             return pl.ds(pl.multiple_of(k * 16, 16), 16)
 
-        @pl.loop(1, NTGT)
-        def _(d):
-            t = tgt_peer(d)
-            to(mkeep.at[r, lot(t), :], tgt1.at[r, ti], ar_send.at[1, r], ar_recv.at[1, r], si, t).start()
-
-        send_images(((0, 2), (2, 0), (2, 2)))
+        mhold[r] = mm(sblk_s[theirs, :], plan[...]).astype(BF16)
+        for way in (2, 1, 3, 0):
+            y = beside(ty, way)
+            to(mhold.at[r, slot64(y), :], sib1.at[r, slot64(y), :], ar_send.at[0, r], pair_recv.at[r, y], sibling, ti).start()
+        gbuf[0:256, :] = mm(sblk_s[ours, :], plan[...])
+        for way in (2, 1, 3, 0):
+            y = beside(ty, way)
+            land = sib1.at[r, slot64(y), :]
+            pltpu.make_async_copy(land, land, pair_recv.at[r, y]).wait()
+            mkeep[r, slot64(y), :] = (gbuf[slot64(y), :] + sib1[r, slot64(y), :].astype(F32)).astype(BF16)
+            for dx in (2, 1, 3, 0):
+                if way == 0 and dx == 0:
+                    continue
+                t = 4 * y + beside(tx, dx)
+                to(mkeep.at[r, lot(t), :], tgt1.at[r, ti], ar_send.at[1, r], ar_recv.at[1, r], si, t).start()
+
+        from_stage((0, 2))
+        send_images(((1, 3), (3, 1)))
         tgt1[r, ti] = mkeep[r, lot(ti), :]
         most = tgt1.at[r, pl.ds(0, NTGT - 1)]
         pltpu.make_async_copy(most, most, ar_recv.at[1, r]).wait()
@@ -385,18 +405,25 @@
         pltpu.make_async_copy(most_z, most_z, ar_recv.at[2, r]).wait()
         mhalf[r, lot(ti), :] = jnp.sum(zred[r].astype(F32), axis=0).astype(BF16)
 
-        @pl.loop(1, NTGT)
-        def _(d):
-            to(mhalf.at[r, lot(ti), :], mhalf.at[r, lot(ti), :], ar_send.at[3, r], ar_recv.at[3, r],
-               si, tgt_peer(d)).start()
-
-        send_images(((1, 2), (3, 2), (2, 1), (2, 3)))
-        most_h = mhalf.at[r, pl.ds(0, 240), :]
-        pltpu.make_async_copy(most_h, most_h, ar_recv.at[3, r]).wait()
-        back = to(mhalf.at[r], mother.at[r], ar_send.at[4, r], ar_recv.at[4, r], sibling, ti)
-        back.start()
+        for dy, dx in FAR_FIRST:
+            t = 4 * beside(ty, dy) + beside(tx, dx)
+            to(mhalf.at[r, lot(ti), :], mhalf.at[r, lot(ti), :], ar_send.at[3, r], lot_recv.at[r, ti], si, t).start()
+
+        def share(land):
+            to(land, mother.at[r, lot_at, :], ar_send.at[4, r], ar_recv.at[4, r], sibling, ti).start()
+
+        lot_at = lot(ti)
+        share(mhalf.at[r, lot_at, :])
+        from_stage((1, 3))
+        send_images(((3, 3), (0, 2), (2, 0), (2, 2)))
+        for dy, dx in FAR_FIRST[::-1]:
+            t = 4 * beside(ty, dy) + beside(tx, dx)
+            lot_at = lot(t)
+            land = mhalf.at[r, lot_at, :]
+            pltpu.make_async_copy(land, land, lot_recv.at[r, t]).wait()
+            share(land)
         gbuf[ours, :] = mhalf[r].astype(F32)
-        back.wait_recv()
+        pltpu.make_async_copy(mother.at[r], mother.at[r], ar_recv.at[4, r]).wait()
         gbuf[theirs, :] = mother[r].astype(F32)
 
         cross = gbuf[...]
@@ -412,8 +439,8 @@
 
         @pl.when(jnp.logical_not(final))
         def _():
-            for part, piece in enumerate(split3(cur[...])):
-                w3[part * D:(part + 1) * D, :] = piece
+            for part, piece in enumerate(split2(cur[...])):
+                w2[part * D:(part + 1) * D, :] = piece
 
         for slot in (2 * r, 2 * r + 1):
             seven = colx.at[slot, pl.ds(0, NSRC - 1)]
@@ -421,11 +448,12 @@
             for half in range(2):
                 most_r = row_most(slot, half)
                 pltpu.make_async_copy(most_r, most_r, row_send_sem.at[slot, half]).wait()
-        pair.wait_send()
+        pltpu.make_async_copy(mhold.at[r], mhold.at[r], ar_send.at[0, r]).wait()
         pltpu.make_async_copy(most, most, ar_send.at[1, r]).wait()
         pltpu.make_async_copy(most_z, most_z, ar_send.at[2, r]).wait()
+        most_h = mhalf.at[r, pl.ds(0, 240), :]
         pltpu.make_async_copy(most_h, most_h, ar_send.at[3, r]).wait()
-        back.wait_send()
+        pltpu.make_async_copy(mother.at[r], mother.at[r], ar_send.at[4, r]).wait()
 
     aligned[...] = 0.5 * cur[...]
     mvx[slot64(ti), :] = plan[slot64(ti), :]
@@ -449,6 +477,7 @@
             moved[64 * part:64 * (part + 1), 128 * cut:128 * (cut + 1)] = total[cut]
 
     pltpu.make_async_copy(most_mv, most_mv, mv_send).wait()
+    pltpu.make_async_copy(stage, stage, st_send).wait()
     pltpu.make_async_copy(most_tgt, most_tgt, tgt_send).wait()
     most_src = sblk.at[pl.ds(0, ROWS - OWN), :]
     pltpu.make_async_copy(most_src, most_src, src_send).wait()
@@ -470,15 +499,18 @@
             v((COLS, D), BF16),
             v((ROWS, COLS), F32),
             v((ROWS, D), BF16),
-            v((ROWS, D), BF16),
+            v((D, ROWS), BF16),
             v((CH, COLS), BF16),
+            v((CH, COLS), BF16),
+            v((CH, 128), F32),
+            v((CH, 128), F32),
             v((ROWS, 128), F32),
             v((ROWS, 128), F32),
             v((ROWS, 128), F32),
             v((8, COLS), F32),
             v((8, COLS), F32),
             v((8, COLS), F32),
-            v((3 * D, D), BF16),
+            v((2 * D, D), BF16),
             v((D, D), F32),
             v((4, NSRC, 8, 128), F32),
             v((4, NTGT, 16, 128), F32),
@@ -492,9 +524,10 @@
             v((2, 256, D), BF16),
             v((2, 256, D), BF16),
             v((16, 128), F32),
+            v((4, OWN, D), BF16),
             dma(()), dma((5, 2)), dma((5, 2)), dma(()), dma((4,)),
             dma((4,)), dma((4,)), dma((4, 2)), dma((4, 2)),
-            dma((5, 2)), dma((5, 2)), dma(()), dma(()),
+            dma((5, 2)), dma((5, 2)), dma(()), dma(()), dma(()), dma((4,)), dma((2, 4)), dma((2, NTGT)),
         ],
         compiler_params=pltpu.CompilerParams(
             collective_id=0, has_side_effects=True, vmem_limit_bytes=48 * 1024 * 1024),

time: 152 us -> 154 us (1.013)
  Pallas kernels: 144 us -> 146 us
where the time goes in v4:
time: 154 us; the launch traced here: 151 us
  Pallas kernels  146 us (95%)
  local copies, waits for them, and re-layouts  3.03 us (2%)
  other arithmetic  1.79 us (1%)
    pallas_call x1, Pallas kernels, shards(): pl.pallas_call(kernel, out_shape=(jax.ShapeDtypeStruct((D, D), F32), jax....  146 us

profile of v4, /device:TPU:8, one launch (start us, length us, event | category | flops | bytes accessed | tf_op | source)
XLA Modules:
  0.0 151.2 jit_solution(7668556009423721921)
XLA Ops:
  0.6 0.0 copy-start
  0.6 1.2 copy-done
  1.9 0.0 copy-start.1
  1.9 0.9 copy-done.1
  2.8 0.0 copy-start.2
  2.8 0.9 copy-done.2
  3.7 145.7 %shard_map.50 = (f32[512,512]{1,0:T(8,128)S(1)}, f32[128,512]{1,0:T(8,128)S(1)}) custom-call(bf16[128,512]{1,0:T(8,128)(2,1)S(1)} %copy-done.1, bf16[64,1024]{1,0:T(8,128)(2,1)S(1)} %bitcast.1, f32[512,512]{1,0:T(8,128)S(1)} %copy-done), custom_call_target="tpu_custom_call" | custom-call | tf_op jit(solution)/shard_map/pallas_call | solution.py:490
  149.4 1.1 broadcast_multiply_fusion
  150.5 0.7 broadcast_multiply_fusion.1
Async XLA Ops:
  0.6 1.2 copy-start
  1.9 0.9 copy-start.1
  2.8 0.9 copy-start.2

commit v5 on v4

--- a/solution.py
+++ b/solution.py
@@ -10,7 +10,6 @@
 
 ROUNDS = 2
 MESH = pl.DeviceIdType.MESH
-VIA = (((1, 2), (0, 3)), ((3, 2), (0, 3)), ((2, 1), (3, 0)), ((2, 3), (3, 0)))
 FAR_FIRST = ((2, 2), (1, 2), (3, 2), (2, 1), (2, 3), (1, 1), (3, 3), (1, 3), (3, 1), (0, 2), (2, 0), (0, 1), (0, 3), (1, 0), (3, 0))
 F32, BF16 = jnp.float32, jnp.bfloat16
 NSRC, NTGT = 8, 16
@@ -36,9 +35,9 @@
 def kernel(
     src_in, tgt_in, rot_in, aligned, moved,
     sblk, sblk_t, feats_t, feats, scores, plan, sblk_s, probs_a, probs_b, parts_a, parts_b, ucol, mrow, lrow,
-    col_m, col_s, vrow, w2, cur, colx, rowx, sib1, tgt1, zred, mhalf, mother, gbuf, mvx, mhold, mkeep, rlse, stage,
+    col_m, col_s, vrow, w2, cur, colx, rowx, sib1, tgt1, zred, mhalf, mother, gbuf, mvb, mvacc, ring1, ring2, ring3, ring4, mhold, mkeep, rlse,
     src_send, near, far, tgt_send, tgt_recv, col_send, col_recv, row_send_sem, row_recv,
-    ar_send, ar_recv, mv_send, mv_recv, st_send, st_recv, pair_recv, lot_recv,
+    ar_send, ar_recv, mv_send, mv_recv,
 ):
     si, ti = lax.axis_index("src"), lax.axis_index("tgt")
     core, zed = lax.rem(si, 2), si // 2
@@ -242,6 +241,15 @@
     def row_expanded(k):
         row = rlse[pl.ds(k, 1), :]
         return jnp.transpose(jnp.broadcast_to(row, (128, 128)))
+
+    kinds = ((0, ty, y_ways, tx, x_ways), (1, tx, x_ways, ty, y_ways))
+
+    def span(at, count):
+        return pl.ds(pl.multiple_of(at, count), count)
+
+    def arrived(step, kind, side, ring):
+        land = ring.at[kind, side]
+        pltpu.make_async_copy(land, land, mv_recv.at[step, kind, side]).wait()
 
     @pl.loop(0, ROUNDS)
     def _(r):
@@ -331,36 +339,6 @@
             pl.loop(half * ROWS // CH // 4, (half + 1) * ROWS // CH // 4)(images)
             row_send(2 * r + 1, half, True)
 
-        def send_images(offsets):
-            @pl.when(final)
-            def _():
-                for dy, dx in offsets:
-                    y, x = beside(ty, dy), beside(tx, dx)
-                    for src, dst in ((4 * y + x, ti), (16 + 4 * x + y, 16 + ti)):
-                        to(plan.at[slot64(src), :], mvx.at[slot64(dst), :], mv_send, mv_recv, si, 4 * y + x).start()
-
-        def to_stage():
-            @pl.when(final)
-            def _():
-                for q, ((dy, dx), (sy, sx)) in enumerate(VIA):
-                    y, x = beside(ty, dy), beside(tx, dx)
-                    for half, src in enumerate((4 * y + x, 16 + 4 * x + y)):
-                        to(plan.at[slot64(src), :], stage.at[q, pl.ds(64 * half, 64), :], st_send, st_recv.at[q],
-                           si, 4 * beside(ty, sy) + beside(tx, sx)).start()
-
-        def from_stage(chosen):
-            @pl.when(final)
-            def _():
-                for q in chosen:
-                    (dy, dx), (sy, sx) = VIA[q]
-                    pltpu.make_async_copy(stage.at[q], stage.at[q], st_recv.at[q]).wait()
-                    sender = 4 * beside(ty, 4 - sy) + beside(tx, 4 - sx)
-                    t = 4 * beside(ty, 4 + dy - sy) + beside(tx, 4 + dx - sx)
-                    for half, dst in enumerate((sender, 16 + sender)):
-                        to(stage.at[q, pl.ds(64 * half, 64), :], mvx.at[slot64(dst), :], mv_send, mv_recv, si, t).start()
-
-        to_stage()
-        send_images(((0, 1), (1, 0), (1, 1), (0, 3), (3, 0)))
         for half in range(2):
             row_combine(2 * r + 1, half)
             factor = jnp.exp2(rowx[2 * r + 1, ti, 8 * half:8 * half + 8, :] - rlse[8 * half:8 * half + 8, :])
@@ -368,29 +346,47 @@
                 lane = slice(128 * (8 * half + k), 128 * (8 * half + k + 1))
                 sblk_s[:, lane] = (sblk_t[:, lane].astype(F32) * factor[k:k + 1, :]).astype(BF16)
 
+        @pl.when(final)
+        def _():
+            for k in range(NTGT):
+                rows = slot128(k)
+                row = jnp.exp2(rowx[2 * r + 1, ti, k:k + 1, :] - rlse[k:k + 1, :])
+                factor = jnp.transpose(jnp.broadcast_to(row, (128, 128)))
+                for cut in range(D // 128):
+                    lane = slice(128 * cut, 128 * (cut + 1))
+                    mvb[rows, lane] = (plan[rows, lane].astype(F32) * factor).astype(BF16)
+            for kind, c, ways, _c, _w in kinds:
+                for side in range(2):
+                    part = mvb.at[span(1024 * kind + 256 * beside(c, 2) + 128 * side, 128), :]
+                    to(part, ring1.at[kind, side], mv_send.at[0], mv_recv.at[0, kind, side], *ways[side]).start()
+
         theirs = pl.ds(pl.multiple_of((1 - core) * 256, 256), 256)
         ours = pl.ds(pl.multiple_of(core * 256, 256), 256)
+        mhold[r] = mm(sblk_s[theirs, :], plan[...]).astype(BF16)
+        pair = to(mhold.at[r], sib1.at[r], ar_send.at[0, r], ar_recv.at[0, r], sibling, ti)
+        pair.start()
+        mine = mm(sblk_s[ours, :], plan[...])
+        pair.wait_recv()
+        mkeep[r] = (mine + sib1[r].astype(F32)).astype(BF16)
+
         def lot(k):
             return pl.ds(pl.multiple_of(k * 16, 16), 16)
 
-        mhold[r] = mm(sblk_s[theirs, :], plan[...]).astype(BF16)
-        for way in (2, 1, 3, 0):
-            y = beside(ty, way)
-            to(mhold.at[r, slot64(y), :], sib1.at[r, slot64(y), :], ar_send.at[0, r], pair_recv.at[r, y], sibling, ti).start()
-        gbuf[0:256, :] = mm(sblk_s[ours, :], plan[...])
-        for way in (2, 1, 3, 0):
-            y = beside(ty, way)
-            land = sib1.at[r, slot64(y), :]
-            pltpu.make_async_copy(land, land, pair_recv.at[r, y]).wait()
-            mkeep[r, slot64(y), :] = (gbuf[slot64(y), :] + sib1[r, slot64(y), :].astype(F32)).astype(BF16)
-            for dx in (2, 1, 3, 0):
-                if way == 0 and dx == 0:
-                    continue
-                t = 4 * y + beside(tx, dx)
-                to(mkeep.at[r, lot(t), :], tgt1.at[r, ti], ar_send.at[1, r], ar_recv.at[1, r], si, t).start()
-
-        from_stage((0, 2))
-        send_images(((1, 3), (3, 1)))
+        for dy, dx in FAR_FIRST:
+            t = 4 * beside(ty, dy) + beside(tx, dx)
+            to(mkeep.at[r, lot(t), :], tgt1.at[r, ti], ar_send.at[1, r], ar_recv.at[1, r], si, t).start()
+
+        @pl.when(final)
+        def _():
+            for kind, c, ways, _c, _w in kinds:
+                for side in range(2):
+                    arrived(0, kind, side, ring1)
+                    unit = 1024 * kind + 256 * beside(c, 1 + 2 * side)
+                    rows = span(unit + 128 * side, 128)
+                    mvb[rows, :] = (mvb[rows, :].astype(F32) + ring1[kind, side].astype(F32)).astype(BF16)
+                    to(mvb.at[span(unit, 256), :], ring2.at[kind, side], mv_send.at[1], mv_recv.at[1, kind, side],
+                       *ways[side]).start()
+
         tgt1[r, ti] = mkeep[r, lot(ti), :]
         most = tgt1.at[r, pl.ds(0, NTGT - 1)]
         pltpu.make_async_copy(most, most, ar_recv.at[1, r]).wait()
@@ -407,23 +403,37 @@
 
         for dy, dx in FAR_FIRST:
             t = 4 * beside(ty, dy) + beside(tx, dx)
-            to(mhalf.at[r, lot(ti), :], mhalf.at[r, lot(ti), :], ar_send.at[3, r], lot_recv.at[r, ti], si, t).start()
-
-        def share(land):
-            to(land, mother.at[r, lot_at, :], ar_send.at[4, r], ar_recv.at[4, r], sibling, ti).start()
-
-        lot_at = lot(ti)
-        share(mhalf.at[r, lot_at, :])
-        from_stage((1, 3))
-        send_images(((3, 3), (0, 2), (2, 0), (2, 2)))
-        for dy, dx in FAR_FIRST[::-1]:
-            t = 4 * beside(ty, dy) + beside(tx, dx)
-            lot_at = lot(t)
-            land = mhalf.at[r, lot_at, :]
-            pltpu.make_async_copy(land, land, lot_recv.at[r, t]).wait()
-            share(land)
+            to(mhalf.at[r, lot(ti), :], mhalf.at[r, lot(ti), :], ar_send.at[3, r], ar_recv.at[3, r], si, t).start()
+
+        @pl.when(final)
+        def _():
+            for kind, c, _w, c2, ways2 in kinds:
+                arrived(1, kind, 0, ring2)
+                arrived(1, kind, 1, ring2)
+                own = mvb[span(1024 * kind + 256 * c, 256), :].astype(F32)
+                mvacc[kind] = (own + ring2[kind, 0].astype(F32) + ring2[kind, 1].astype(F32)).astype(BF16)
+                for side in range(2):
+                    part = mvacc.at[kind, span(64 * beside(c2, 2) + 32 * side, 32), :]
+                    to(part, ring3.at[kind, side], mv_send.at[2], mv_recv.at[2, kind, side], *ways2[side]).start()
+
+        most_h = mhalf.at[r, pl.ds(0, 240), :]
+        pltpu.make_async_copy(most_h, most_h, ar_recv.at[3, r]).wait()
+        back = to(mhalf.at[r], mother.at[r], ar_send.at[4, r], ar_recv.at[4, r], sibling, ti)
+        back.start()
         gbuf[ours, :] = mhalf[r].astype(F32)
-        pltpu.make_async_copy(mother.at[r], mother.at[r], ar_recv.at[4, r]).wait()
+
+        @pl.when(final)
+        def _():
+            for kind, _c, _w, c2, ways2 in kinds:
+                for side in range(2):
+                    arrived(2, kind, side, ring3)
+                    block = 64 * beside(c2, 1 + 2 * side)
+                    rows = span(block + 32 * side, 32)
+                    mvacc[kind, rows, :] = (mvacc[kind, rows, :].astype(F32) + ring3[kind, side].astype(F32)).astype(BF16)
+                    to(mvacc.at[kind, span(block, 64), :], ring4.at[kind, side], mv_send.at[3],
+                       mv_recv.at[3, kind, side], *ways2[side]).start()
+
+        back.wait_recv()
         gbuf[theirs, :] = mother[r].astype(F32)
 
         cross = gbuf[...]
@@ -448,36 +458,20 @@
             for half in range(2):
                 most_r = row_most(slot, half)
                 pltpu.make_async_copy(most_r, most_r, row_send_sem.at[slot, half]).wait()
-        pltpu.make_async_copy(mhold.at[r], mhold.at[r], ar_send.at[0, r]).wait()
+        pair.wait_send()
         pltpu.make_async_copy(most, most, ar_send.at[1, r]).wait()
         pltpu.make_async_copy(most_z, most_z, ar_send.at[2, r]).wait()
-        most_h = mhalf.at[r, pl.ds(0, 240), :]
         pltpu.make_async_copy(most_h, most_h, ar_send.at[3, r]).wait()
-        pltpu.make_async_copy(mother.at[r], mother.at[r], ar_send.at[4, r]).wait()
+        back.wait_send()
 
     aligned[...] = 0.5 * cur[...]
-    mvx[slot64(ti), :] = plan[slot64(ti), :]
-    mvx[slot64(16 + ti), :] = plan[slot64(16 + across), :]
-    most_mv = mvx.at[pl.ds(0, ROWS - OWN), :]
-    pltpu.make_async_copy(most_mv, most_mv, mv_recv).wait()
-    for part, place in ((0, ti), (1, across)):
-        stat = 8 * part + place // 2
-        odd = lax.rem(place, 2) == 1
-        whole = rlse[pl.ds(stat, 1), :]
-        total = [0.0] * (D // 128)
-        for k in range(NTGT):
-            share = 0.5 * jnp.exp2(rowx[2 * ROUNDS - 1, k, pl.ds(stat, 1), :] - whole)
-            factor = jnp.transpose(jnp.broadcast_to(share, (128, 128)))
-            factor = jnp.where(odd, factor[64:128], factor[0:64])
-            at = (16 * part + k) * 64
-            for cut in range(D // 128):
-                lane = slice(128 * cut, 128 * (cut + 1))
-                total[cut] = total[cut] + mvx[at:at + 64, lane].astype(F32) * factor
-        for cut in range(D // 128):
-            moved[64 * part:64 * (part + 1), 128 * cut:128 * (cut + 1)] = total[cut]
-
-    pltpu.make_async_copy(most_mv, most_mv, mv_send).wait()
-    pltpu.make_async_copy(stage, stage, st_send).wait()
+    for kind, _c, _w, c2, _w2 in kinds:
+        arrived(3, kind, 0, ring4)
+        arrived(3, kind, 1, ring4)
+        own = mvacc[kind, span(64 * c2, 64), :].astype(F32)
+        moved[64 * kind:64 * (kind + 1), :] = 0.5 * (own + ring4[kind, 0].astype(F32) + ring4[kind, 1].astype(F32))
+    for step, ring in enumerate((ring1, ring2, ring3, ring4)):
+        pltpu.make_async_copy(ring, ring, mv_send.at[step]).wait()
     pltpu.make_async_copy(most_tgt, most_tgt, tgt_send).wait()
     most_src = sblk.at[pl.ds(0, ROWS - OWN), :]
     pltpu.make_async_copy(most_src, most_src, src_send).wait()
@@ -522,12 +516,16 @@
             v((D, D), F32),
             v((ROWS, D), BF16),
             v((2, 256, D), BF16),
+            v((2, 2, 128, D), BF16),
+            v((2, 2, 256, D), BF16),
+            v((2, 2, 32, D), BF16),
+            v((2, 2, 64, D), BF16),
+            v((2, 256, D), BF16),
             v((2, 256, D), BF16),
             v((16, 128), F32),
-            v((4, OWN, D), BF16),
             dma(()), dma((5, 2)), dma((5, 2)), dma(()), dma((4,)),
             dma((4,)), dma((4,)), dma((4, 2)), dma((4, 2)),
-            dma((5, 2)), dma((5, 2)), dma(()), dma(()), dma(()), dma((4,)), dma((2, 4)), dma((2, NTGT)),
+            dma((5, 2)), dma((5, 2)), dma((4,)), dma((4, 2, 2)),
         ],
         compiler_params=pltpu.CompilerParams(
             collective_id=0, has_side_effects=True, vmem_limit_bytes=48 * 1024 * 1024),

time: 154 us -> 137 us (0.89)
  Pallas kernels: 146 us -> 129 us
    pallas_call x1, Pallas kernels: 146 us -> 129 us  [shards(): pl.pallas_call(kernel, out_shape=(jax.ShapeDtypeStruct((D, D), F32), jax....]
where the time goes in v5:
time: 137 us; the launch traced here: 135 us
  Pallas kernels  129 us (94%)
  local copies, waits for them, and re-layouts  3.03 us (2%)
  other arithmetic  1.79 us (1%)
    pallas_call x1, Pallas kernels, shards(): pl.pallas_call(kernel, out_shape=(jax.ShapeDtypeStruct((D, D), F32), jax....  129 us
    unnamed x6, local copies, waits for them, and re-layouts  3.03 us

profile of v5, /device:TPU:8, one launch (start us, length us, event | category | flops | bytes accessed | tf_op | source)
XLA Modules:
  0.0 134.8 jit_solution(370231923135054673)
XLA Ops:
  0.6 0.0 copy-start
  0.6 1.2 copy-done
  1.9 0.0 copy-start.1
  1.9 0.9 copy-done.1
  2.8 0.0 copy-start.2
  2.8 0.9 copy-done.2
  3.7 129.3 %shard_map.50 = (f32[512,512]{1,0:T(8,128)S(1)}, f32[128,512]{1,0:T(8,128)S(1)}) custom-call(bf16[128,512]{1,0:T(8,128)(2,1)S(1)} %copy-done.1, bf16[64,1024]{1,0:T(8,128)(2,1)S(1)} %bitcast.1, f32[512,512]{1,0:T(8,128)S(1)} %copy-done), custom_call_target="tpu_custom_call" | custom-call | tf_op jit(solution)/shard_map/pallas_call | solution.py:484
  133.0 1.1 broadcast_multiply_fusion
  134.1 0.7 broadcast_multiply_fusion.1
Async XLA Ops:
  0.6 1.2 copy-start
  1.9 0.9 copy-start.1
  2.8 0.9 copy-start.2

commit v6 on v5

--- a/solution.py
+++ b/solution.py
@@ -34,7 +34,7 @@
 
 def kernel(
     src_in, tgt_in, rot_in, aligned, moved,
-    sblk, sblk_t, feats_t, feats, scores, plan, sblk_s, probs_a, probs_b, parts_a, parts_b, ucol, mrow, lrow,
+    sblk, sblk_t, feats_t, feats, scores, plan, sblk_s, probs, tops_row, ucol, mrow, lrow,
     col_m, col_s, vrow, w2, cur, colx, rowx, sib1, tgt1, zred, mhalf, mother, gbuf, mvb, mvacc, ring1, ring2, ring3, ring4, mhold, mkeep, rlse,
     src_send, near, far, tgt_send, tgt_recv, col_send, col_recv, row_send_sem, row_recv,
     ar_send, ar_recv, mv_send, mv_recv,
@@ -61,6 +61,16 @@
     def _(d):
         pl.semaphore_signal(barrier, inc=1, device_id=(src_peer(d), ti), device_id_type=MESH)
 
+    def slot64(k):
+        return pl.ds(pl.multiple_of(k * 64, 64), 64)
+
+    sblk[slot64(ti), :] = src_in[0:64, :]
+    sblk[slot64(16 + across), :] = src_in[64:128, :]
+    feats_t[slot64(si), :] = tgt_in[...]
+    cur[...] = rot_in[...]
+    for part, piece in enumerate(split2(rot_in[...])):
+        w2[part * D:(part + 1) * D, :] = piece
+
     pl.semaphore_wait(barrier, NTGT + NSRC - 2)
 
     def to(src, dst, send, recv, s, t):
@@ -70,9 +80,6 @@
 
     def slot128(k):
         return pl.ds(pl.multiple_of(k * OWN, OWN), OWN)
-
-    def slot64(k):
-        return pl.ds(pl.multiple_of(k * 64, 64), 64)
 
     def beside(c, d):
         return lax.rem(c + d, 4)
@@ -113,12 +120,6 @@
     both_ways(4, lower, own_low, x_ways, src_send)
     to(tgt_in, own_feats, tgt_send, tgt_recv.at[zed], sibling, ti).start()
 
-    sblk[slot64(ti), :] = src_in[0:64, :]
-    sblk[slot64(16 + across), :] = src_in[64:128, :]
-    feats_t[slot64(si), :] = tgt_in[...]
-    cur[...] = rot_in[...]
-    for part, piece in enumerate(split2(rot_in[...])):
-        w2[part * D:(part + 1) * D, :] = piece
 
     def up_on(land, k):
         both_ways(3, land, land, y_ways, src_send)
@@ -148,8 +149,6 @@
         land = feats_t.at[slot64(2 * k + 1 - core), :]
         pltpu.make_async_copy(land, land, tgt_recv.at[k]).wait()
     most_tgt = feats_t.at[pl.ds(0, D - 64), :]
-    for part in range(D // 128):
-        feats[:, 128 * part:128 * (part + 1)] = jnp.transpose(feats_t[128 * part:128 * (part + 1), :])
 
     def chunk(j):
         return pl.ds(pl.multiple_of(j * CH, CH), CH)
@@ -170,7 +169,7 @@
             col_s[:, cut] = col_s[:, cut] * jnp.exp2(old - new) + jnp.sum(jnp.exp2(x - new[None]), axis=0)
             col_m[:, cut] = new
 
-    def col_exchange(slot):
+    def col_start(slot):
         for ct in range(COLS // 128):
             cut = pl.ds(128 * ct, 128)
             high = jnp.max(col_m[:, cut], axis=0, keepdims=True)
@@ -181,6 +180,7 @@
             s = 2 * beside(zed, d // 2) + lax.rem(core + d, 2)
             to(colx.at[slot, si], colx.at[slot, si], col_send.at[slot], col_recv.at[slot], s, ti).start()
 
+    def col_finish(slot):
         seven = colx.at[slot, pl.ds(0, NSRC - 1)]
         pltpu.make_async_copy(seven, seven, col_recv.at[slot]).wait()
         every = colx[slot]
@@ -215,7 +215,8 @@
             rows = slot128(k)
             if shared:
                 high = jnp.transpose(mrow[rows, :])[0:1, :]
-                total = jnp.transpose(lrow[rows, :])[0:1, :]
+                total = jnp.sum(jnp.transpose(lrow[rows, :]), axis=0, keepdims=True)
+                tops_row[k:k + 1, :] = high
             else:
                 tops = jnp.transpose(mrow[rows, :])
                 high = jnp.max(tops, axis=0, keepdims=True)
@@ -271,18 +272,22 @@
                 relayed(3, sblk, lambda k: CH * k, CH, ty, nothing)
                 relayed(4, sblk, lambda k: ROWS // 2 + CH * k, CH, tx, nothing)
 
-            @pl.when(first)
-            def _():
-                for rows in pair:
-                    sblk_t[:, rows] = jnp.transpose(sblk[rows, :])
-
             turned = [mm(jnp.concatenate([sblk[rows, :]] * 2, axis=1), w2[...]).astype(BF16) for rows in pair]
             for rows, z in zip(pair, turned):
                 scores[rows, :] = mm(z, feats_t[...]) * SCALE
             for rows in pair:
                 col_update(rows, False)
 
-        col_exchange(2 * r)
+        col_start(2 * r)
+
+        @pl.when(first)
+        def _():
+            for part in range(D // 128):
+                feats[:, 128 * part:128 * (part + 1)] = jnp.transpose(feats_t[128 * part:128 * (part + 1), :])
+            for j in range(ROWS // CH):
+                sblk_t[:, CH * j:CH * (j + 1)] = jnp.transpose(sblk[CH * j:CH * (j + 1), :])
+
+        col_finish(2 * r)
 
         for half in range(2):
             @pl.loop(half * ROWS // RB // 2, (half + 1) * ROWS // RB // 2)
@@ -301,7 +306,8 @@
             def _(j):
                 col_update(chunk(j), True)
 
-        col_exchange(2 * r + 1)
+        col_start(2 * r + 1)
+        col_finish(2 * r + 1)
 
         @pl.loop(0, ROWS // RB)
         def _(step):
@@ -313,52 +319,32 @@
             rows = pl.ds(pl.multiple_of(step * 512, 512), 512)
             mrow[rows, :] = jnp.broadcast_to(jnp.max(mrow[rows, :], axis=1, keepdims=True), (512, 128))
 
-        def images(i):
-            for side, (probs, parts) in enumerate(((probs_a, parts_a), (probs_b, parts_b))):
-                j = 2 * i + side
-                for step in range(CH // RB):
-                    rows = pl.ds(pl.multiple_of(j * CH + step * RB, RB), RB)
+        for half in range(2):
+            @pl.loop(half * ROWS // RB // 4, (half + 1) * ROWS // RB // 4)
+            def _(step):
+                for side in range(2):
+                    rows = pl.ds(pl.multiple_of((2 * step + side) * RB, RB), RB)
                     top = mrow[rows, :]
                     total = None
                     for ct in range(COLS // 128):
                         p = jnp.exp2(row_tile(rows, ct) - top)
                         total = p if total is None else total + p
-                        probs[step * RB:(step + 1) * RB, 128 * ct:128 * (ct + 1)] = p.astype(BF16)
-                    parts[step * RB:(step + 1) * RB, :] = total
-            for side, (probs, parts) in enumerate(((probs_a, parts_a), (probs_b, parts_b))):
-                rows = chunk(2 * i + side)
-                image = mm(probs[...], feats[...])
-                sums = jnp.broadcast_to(jnp.sum(parts[...], axis=1, keepdims=True), (CH, 128))
-                lrow[rows, :] = sums
-                inverse = 1.0 / sums
-                for cut in range(D // 128):
-                    lane = slice(128 * cut, 128 * (cut + 1))
-                    plan[rows, lane] = (image[:, lane] * inverse).astype(BF16)
-
-        for half in range(2):
-            pl.loop(half * ROWS // CH // 4, (half + 1) * ROWS // CH // 4)(images)
+                        probs[rows, 128 * ct:128 * (ct + 1)] = p.astype(BF16)
+                    lrow[rows, :] = total
+
             row_send(2 * r + 1, half, True)
+
+        @pl.loop(0, ROWS // 512)
+        def _(step):
+            rows = pl.ds(pl.multiple_of(step * 512, 512), 512)
+            plan[rows, :] = mm(probs[rows, :], feats[...]).astype(BF16)
 
         for half in range(2):
             row_combine(2 * r + 1, half)
-            factor = jnp.exp2(rowx[2 * r + 1, ti, 8 * half:8 * half + 8, :] - rlse[8 * half:8 * half + 8, :])
+            factor = jnp.exp2(tops_row[8 * half:8 * half + 8, :] - rlse[8 * half:8 * half + 8, :])
             for k in range(8):
                 lane = slice(128 * (8 * half + k), 128 * (8 * half + k + 1))
                 sblk_s[:, lane] = (sblk_t[:, lane].astype(F32) * factor[k:k + 1, :]).astype(BF16)
-
-        @pl.when(final)
-        def _():
-            for k in range(NTGT):
-                rows = slot128(k)
-                row = jnp.exp2(rowx[2 * r + 1, ti, k:k + 1, :] - rlse[k:k + 1, :])
-                factor = jnp.transpose(jnp.broadcast_to(row, (128, 128)))
-                for cut in range(D // 128):
-                    lane = slice(128 * cut, 128 * (cut + 1))
-                    mvb[rows, lane] = (plan[rows, lane].astype(F32) * factor).astype(BF16)
-            for kind, c, ways, _c, _w in kinds:
-                for side in range(2):
-                    part = mvb.at[span(1024 * kind + 256 * beside(c, 2) + 128 * side, 128), :]
-                    to(part, ring1.at[kind, side], mv_send.at[0], mv_recv.at[0, kind, side], *ways[side]).start()
 
         theirs = pl.ds(pl.multiple_of((1 - core) * 256, 256), 256)
         ours = pl.ds(pl.multiple_of(core * 256, 256), 256)
@@ -366,6 +352,16 @@
         pair = to(mhold.at[r], sib1.at[r], ar_send.at[0, r], ar_recv.at[0, r], sibling, ti)
         pair.start()
         mine = mm(sblk_s[ours, :], plan[...])
+        @pl.when(final)
+        def _():
+            for k in range(NTGT):
+                rows = slot128(k)
+                row = jnp.exp2(tops_row[k:k + 1, :] - rlse[k:k + 1, :])
+                factor = jnp.transpose(jnp.broadcast_to(row, (128, 128)))
+                for cut in range(D // 128):
+                    lane = slice(128 * cut, 128 * (cut + 1))
+                    mvb[rows, lane] = (plan[rows, lane].astype(F32) * factor).astype(BF16)
+
         pair.wait_recv()
         mkeep[r] = (mine + sib1[r].astype(F32)).astype(BF16)
 
@@ -375,6 +371,23 @@
         for dy, dx in FAR_FIRST:
             t = 4 * beside(ty, dy) + beside(tx, dx)
             to(mkeep.at[r, lot(t), :], tgt1.at[r, ti], ar_send.at[1, r], ar_recv.at[1, r], si, t).start()
+
+        @pl.when(final)
+        def _():
+            for kind, c, ways, _c, _w in kinds:
+                for side in range(2):
+                    part = mvb.at[span(1024 * kind + 256 * beside(c, 2) + 128 * side, 128), :]
+                    to(part, ring1.at[kind, side], mv_send.at[0], mv_recv.at[0, kind, side], *ways[side]).start()
+
+        tgt1[r, ti] = mkeep[r, lot(ti), :]
+        most = tgt1.at[r, pl.ds(0, NTGT - 1)]
+        pltpu.make_async_copy(most, most, ar_recv.at[1, r]).wait()
+        zred[r, zed] = jnp.sum(tgt1[r].astype(F32), axis=0).astype(BF16)
+
+        @pl.loop(1, 4)
+        def _(d):
+            other = lax.rem(zed + d, 4) * 2 + core
+            to(zred.at[r, zed], zred.at[r, zed], ar_send.at[2, r], ar_recv.at[2, r], other, ti).start()
 
         @pl.when(final)
         def _():
@@ -386,16 +399,6 @@
                     mvb[rows, :] = (mvb[rows, :].astype(F32) + ring1[kind, side].astype(F32)).astype(BF16)
                     to(mvb.at[span(unit, 256), :], ring2.at[kind, side], mv_send.at[1], mv_recv.at[1, kind, side],
                        *ways[side]).start()
-
-        tgt1[r, ti] = mkeep[r, lot(ti), :]
-        most = tgt1.at[r, pl.ds(0, NTGT - 1)]
-        pltpu.make_async_copy(most, most, ar_recv.at[1, r]).wait()
-        zred[r, zed] = jnp.sum(tgt1[r].astype(F32), axis=0).astype(BF16)
-
-        @pl.loop(1, 4)
-        def _(d):
-            other = lax.rem(zed + d, 4) * 2 + core
-            to(zred.at[r, zed], zred.at[r, zed], ar_send.at[2, r], ar_recv.at[2, r], other, ti).start()
 
         most_z = zred.at[r, pl.ds(0, 3)]
         pltpu.make_async_copy(most_z, most_z, ar_recv.at[2, r]).wait()
@@ -494,10 +497,8 @@
             v((ROWS, COLS), F32),
             v((ROWS, D), BF16),
             v((D, ROWS), BF16),
-            v((CH, COLS), BF16),
-            v((CH, COLS), BF16),
-            v((CH, 128), F32),
-            v((CH, 128), F32),
+            v((ROWS, COLS), BF16),
+            v((16, 128), F32),
             v((ROWS, 128), F32),
             v((ROWS, 128), F32),
             v((ROWS, 128), F32),

time: 137 us -> 138 us (level); the launches traced: 135 us -> 138 us
  Pallas kernels: 129 us -> 132 us
    pallas_call x1, Pallas kernels: 129 us -> 132 us  [shards(): pl.pallas_call(kernel, out_shape=(jax.ShapeDtypeStruct((D, D), F32), jax....]
where the time goes in v6:
time: 138 us
  Pallas kernels  132 us (96%)
  local copies, waits for them, and re-layouts  3.03 us (2%)
  other arithmetic  1.79 us (1%)
    pallas_call x1, Pallas kernels, shards(): pl.pallas_call(kernel, out_shape=(jax.ShapeDtypeStruct((D, D), F32), jax....  132 us
    unnamed x6, local copies, waits for them, and re-layouts  3.03 us

profile of v6, /device:TPU:8, one launch (start us, length us, event | category | flops | bytes accessed | tf_op | source)
XLA Modules:
  0.0 137.9 jit_solution(8942258964855709488)
XLA Ops:
  0.6 0.0 copy-start
  0.6 1.2 copy-done
  1.9 0.0 copy-start.1
  1.9 0.9 copy-done.1
  2.8 0.0 copy-start.2
  2.8 0.9 copy-done.2
  3.7 132.5 %shard_map.50 = (f32[512,512]{1,0:T(8,128)S(1)}, f32[128,512]{1,0:T(8,128)S(1)}) custom-call(bf16[128,512]{1,0:T(8,128)(2,1)S(1)} %copy-done.1, bf16[64,1024]{1,0:T(8,128)(2,1)S(1)} %bitcast.1, f32[512,512]{1,0:T(8,128)S(1)} %copy-done), custom_call_target="tpu_custom_call" | custom-call | tf_op jit(solution)/shard_map/pallas_call | solution.py:487
  136.2 1.1 broadcast_multiply_fusion
  137.2 0.7 broadcast_multiply_fusion.1
Async XLA Ops:
  0.6 1.2 copy-start
  1.9 0.9 copy-start.1
  2.8 0.9 copy-start.2

commit v7 on v6

--- a/solution.py
+++ b/solution.py
@@ -346,12 +346,6 @@
                 lane = slice(128 * (8 * half + k), 128 * (8 * half + k + 1))
                 sblk_s[:, lane] = (sblk_t[:, lane].astype(F32) * factor[k:k + 1, :]).astype(BF16)
 
-        theirs = pl.ds(pl.multiple_of((1 - core) * 256, 256), 256)
-        ours = pl.ds(pl.multiple_of(core * 256, 256), 256)
-        mhold[r] = mm(sblk_s[theirs, :], plan[...]).astype(BF16)
-        pair = to(mhold.at[r], sib1.at[r], ar_send.at[0, r], ar_recv.at[0, r], sibling, ti)
-        pair.start()
-        mine = mm(sblk_s[ours, :], plan[...])
         @pl.when(final)
         def _():
             for k in range(NTGT):
@@ -361,33 +355,26 @@
                 for cut in range(D // 128):
                     lane = slice(128 * cut, 128 * (cut + 1))
                     mvb[rows, lane] = (plan[rows, lane].astype(F32) * factor).astype(BF16)
-
-        pair.wait_recv()
-        mkeep[r] = (mine + sib1[r].astype(F32)).astype(BF16)
-
-        def lot(k):
-            return pl.ds(pl.multiple_of(k * 16, 16), 16)
-
-        for dy, dx in FAR_FIRST:
-            t = 4 * beside(ty, dy) + beside(tx, dx)
-            to(mkeep.at[r, lot(t), :], tgt1.at[r, ti], ar_send.at[1, r], ar_recv.at[1, r], si, t).start()
-
-        @pl.when(final)
-        def _():
             for kind, c, ways, _c, _w in kinds:
                 for side in range(2):
                     part = mvb.at[span(1024 * kind + 256 * beside(c, 2) + 128 * side, 128), :]
                     to(part, ring1.at[kind, side], mv_send.at[0], mv_recv.at[0, kind, side], *ways[side]).start()
 
-        tgt1[r, ti] = mkeep[r, lot(ti), :]
-        most = tgt1.at[r, pl.ds(0, NTGT - 1)]
-        pltpu.make_async_copy(most, most, ar_recv.at[1, r]).wait()
-        zred[r, zed] = jnp.sum(tgt1[r].astype(F32), axis=0).astype(BF16)
-
-        @pl.loop(1, 4)
-        def _(d):
-            other = lax.rem(zed + d, 4) * 2 + core
-            to(zred.at[r, zed], zred.at[r, zed], ar_send.at[2, r], ar_recv.at[2, r], other, ti).start()
+        theirs = pl.ds(pl.multiple_of((1 - core) * 256, 256), 256)
+        ours = pl.ds(pl.multiple_of(core * 256, 256), 256)
+        mhold[r] = mm(sblk_s[theirs, :], plan[...]).astype(BF16)
+        pair = to(mhold.at[r], sib1.at[r], ar_send.at[0, r], ar_recv.at[0, r], sibling, ti)
+        pair.start()
+        mine = mm(sblk_s[ours, :], plan[...])
+        pair.wait_recv()
+        mkeep[r] = (mine + sib1[r].astype(F32)).astype(BF16)
+
+        def lot(k):
+            return pl.ds(pl.multiple_of(k * 16, 16), 16)
+
+        for dy, dx in FAR_FIRST:
+            t = 4 * beside(ty, dy) + beside(tx, dx)
+            to(mkeep.at[r, lot(t), :], tgt1.at[r, ti], ar_send.at[1, r], ar_recv.at[1, r], si, t).start()
 
         @pl.when(final)
         def _():
@@ -399,6 +386,16 @@
                     mvb[rows, :] = (mvb[rows, :].astype(F32) + ring1[kind, side].astype(F32)).astype(BF16)
                     to(mvb.at[span(unit, 256), :], ring2.at[kind, side], mv_send.at[1], mv_recv.at[1, kind, side],
                        *ways[side]).start()
+
+        tgt1[r, ti] = mkeep[r, lot(ti), :]
+        most = tgt1.at[r, pl.ds(0, NTGT - 1)]
+        pltpu.make_async_copy(most, most, ar_recv.at[1, r]).wait()
+        zred[r, zed] = jnp.sum(tgt1[r].astype(F32), axis=0).astype(BF16)
+
+        @pl.loop(1, 4)
+        def _(d):
+            other = lax.rem(zed + d, 4) * 2 + core
+            to(zred.at[r, zed], zred.at[r, zed], ar_send.at[2, r], ar_recv.at[2, r], other, ti).start()
 
         most_z = zred.at[r, pl.ds(0, 3)]
         pltpu.make_async_copy(most_z, most_z, ar_recv.at[2, r]).wait()

time: 138 us -> 134 us (0.971); the launches traced: 138 us -> 132 us
  Pallas kernels: 132 us -> 126 us
    pallas_call x1, Pallas kernels: 132 us -> 126 us  [shards(): pl.pallas_call(kernel, out_shape=(jax.ShapeDtypeStruct((D, D), F32), jax....]
where the time goes in v7:
time: 134 us; the launch traced here: 132 us
  Pallas kernels  126 us (94%)
  local copies, waits for them, and re-layouts  3.03 us (2%)
  other arithmetic  1.79 us (1%)
    pallas_call x1, Pallas kernels, shards(): pl.pallas_call(kernel, out_shape=(jax.ShapeDtypeStruct((D, D), F32), jax....  126 us
    unnamed x6, local copies, waits for them, and re-layouts  3.03 us

profile of v7, /device:TPU:8, one launch (start us, length us, event | category | flops | bytes accessed | tf_op | source)
XLA Modules:
  0.0 131.8 jit_solution(16708686624411250145)
XLA Ops:
  0.6 0.0 copy-start
  0.6 1.2 copy-done
  1.9 0.0 copy-start.1
  1.9 0.9 copy-done.1
  2.8 0.0 copy-start.2
  2.8 0.9 copy-done.2
  3.7 126.4 %shard_map.50 = (f32[512,512]{1,0:T(8,128)S(1)}, f32[128,512]{1,0:T(8,128)S(1)}) custom-call(bf16[128,512]{1,0:T(8,128)(2,1)S(1)} %copy-done.1, bf16[64,1024]{1,0:T(8,128)(2,1)S(1)} %bitcast.1, f32[512,512]{1,0:T(8,128)S(1)} %copy-done), custom_call_target="tpu_custom_call" | custom-call | tf_op jit(solution)/shard_map/pallas_call | solution.py:484
  130.1 1.1 broadcast_multiply_fusion
  131.1 0.7 broadcast_multiply_fusion.1
Async XLA Ops:
  0.6 1.2 copy-start
  1.9 0.9 copy-start.1
  2.8 0.9 copy-start.2

commit v8 on v7

--- a/solution.py
+++ b/solution.py
@@ -290,9 +290,10 @@
         col_finish(2 * r)
 
         for half in range(2):
-            @pl.loop(half * ROWS // RB // 2, (half + 1) * ROWS // RB // 2)
+            @pl.loop(half * ROWS // RB // 4, (half + 1) * ROWS // RB // 4)
             def _(step):
-                row_pass(step)
+                row_pass(2 * step)
+                row_pass(2 * step + 1)
 
             row_send(2 * r, half, False)
 
@@ -309,10 +310,11 @@
         col_start(2 * r + 1)
         col_finish(2 * r + 1)
 
-        @pl.loop(0, ROWS // RB)
+        @pl.loop(0, ROWS // RB // 4)
         def _(step):
-            rows = pl.ds(pl.multiple_of(step * RB, RB), RB)
-            mrow[rows, :] = lane_max(rows)
+            for side in range(4):
+                rows = pl.ds(pl.multiple_of((4 * step + side) * RB, RB), RB)
+                mrow[rows, :] = lane_max(rows)
 
         @pl.loop(0, ROWS // 512)
         def _(step):
@@ -345,6 +347,8 @@
             for k in range(8):
                 lane = slice(128 * (8 * half + k), 128 * (8 * half + k + 1))
                 sblk_s[:, lane] = (sblk_t[:, lane].astype(F32) * factor[k:k + 1, :]).astype(BF16)
+            if half == 0:
+                gbuf[...] = mm(sblk_s[:, 0:ROWS // 2], plan[0:ROWS // 2, :])
 
         @pl.when(final)
         def _():
@@ -362,10 +366,10 @@
 
         theirs = pl.ds(pl.multiple_of((1 - core) * 256, 256), 256)
         ours = pl.ds(pl.multiple_of(core * 256, 256), 256)
-        mhold[r] = mm(sblk_s[theirs, :], plan[...]).astype(BF16)
+        mhold[r] = (gbuf[theirs, :] + mm(sblk_s[theirs, ROWS // 2:], plan[ROWS // 2:, :])).astype(BF16)
         pair = to(mhold.at[r], sib1.at[r], ar_send.at[0, r], ar_recv.at[0, r], sibling, ti)
         pair.start()
-        mine = mm(sblk_s[ours, :], plan[...])
+        mine = gbuf[ours, :] + mm(sblk_s[ours, ROWS // 2:], plan[ROWS // 2:, :])
         pair.wait_recv()
         mkeep[r] = (mine + sib1[r].astype(F32)).astype(BF16)
 

time: 134 us -> 130 us (0.970)
  Pallas kernels: 126 us -> 123 us
    pallas_call x1, Pallas kernels: 126 us -> 123 us  [shards(): pl.pallas_call(kernel, out_shape=(jax.ShapeDtypeStruct((D, D), F32), jax....]
where the time goes in v8:
time: 130 us; the launch traced here: 129 us
  Pallas kernels  123 us (95%)
  local copies, waits for them, and re-layouts  3.03 us (2%)
  other arithmetic  1.79 us (1%)
    pallas_call x1, Pallas kernels, shards(): pl.pallas_call(kernel, out_shape=(jax.ShapeDtypeStruct((D, D), F32), jax....  123 us
    unnamed x6, local copies, waits for them, and re-layouts  3.03 us

profile of v8, /device:TPU:8, one launch (start us, length us, event | category | flops | bytes accessed | tf_op | source)
XLA Modules:
  0.0 128.7 jit_solution(11077997414079767951)
XLA Ops:
  0.6 0.0 copy-start
  0.6 1.2 copy-done
  1.9 0.0 copy-start.1
  1.9 0.9 copy-done.1
  2.8 0.0 copy-start.2
  2.8 0.9 copy-done.2
  3.7 123.3 %shard_map.50 = (f32[512,512]{1,0:T(8,128)S(1)}, f32[128,512]{1,0:T(8,128)S(1)}) custom-call(bf16[128,512]{1,0:T(8,128)(2,1)S(1)} %copy-done.1, bf16[64,1024]{1,0:T(8,128)(2,1)S(1)} %bitcast.1, f32[512,512]{1,0:T(8,128)S(1)} %copy-done), custom_call_target="tpu_custom_call" | custom-call | tf_op jit(solution)/shard_map/pallas_call | solution.py:488
  127.0 1.1 broadcast_multiply_fusion
  128.0 0.7 broadcast_multiply_fusion.1
Async XLA Ops:
  0.6 1.2 copy-start
  1.9 0.9 copy-start.1
  2.8 0.9 copy-start.2

commit v9 on v8

--- a/solution.py
+++ b/solution.py
@@ -303,9 +303,10 @@
             for k in range(8 * half, 8 * half + 8):
                 ucol[slot128(k), :] = -LOG_N - row_expanded(k)
 
-            @pl.loop(half * ROWS // CH // 2, (half + 1) * ROWS // CH // 2)
+            @pl.loop(half * ROWS // CH // 4, (half + 1) * ROWS // CH // 4)
             def _(j):
-                col_update(chunk(j), True)
+                col_update(chunk(2 * j), True)
+                col_update(chunk(2 * j + 1), True)
 
         col_start(2 * r + 1)
         col_finish(2 * r + 1)

time: 130 us -> 130 us (level)
  no operation moved by 1% of the time
where the time goes in v9:
time: 130 us; the launch traced here: 129 us
  Pallas kernels  123 us (95%)
  local copies, waits for them, and re-layouts  3.03 us (2%)
  other arithmetic  1.79 us (1%)
    pallas_call x1, Pallas kernels, shards(): pl.pallas_call(kernel, out_shape=(jax.ShapeDtypeStruct((D, D), F32), jax....  123 us
    unnamed x6, local copies, waits for them, and re-layouts  3.03 us

profile of v9, /device:TPU:8, one launch (start us, length us, event | category | flops | bytes accessed | tf_op | source)
XLA Modules:
  0.0 128.7 jit_solution(11938352024414780705)
XLA Ops:
  0.6 0.0 copy-start
  0.6 1.2 copy-done
  1.9 0.0 copy-start.1
  1.9 0.9 copy-done.1
  2.8 0.0 copy-start.2
  2.8 0.9 copy-done.2
  3.7 123.2 %shard_map.50 = (f32[512,512]{1,0:T(8,128)S(1)}, f32[128,512]{1,0:T(8,128)S(1)}) custom-call(bf16[128,512]{1,0:T(8,128)(2,1)S(1)} %copy-done.1, bf16[64,1024]{1,0:T(8,128)(2,1)S(1)} %bitcast.1, f32[512,512]{1,0:T(8,128)S(1)} %copy-done), custom_call_target="tpu_custom_call" | custom-call | tf_op jit(solution)/shard_map/pallas_call | solution.py:489
  126.9 1.1 broadcast_multiply_fusion
  127.9 0.7 broadcast_multiply_fusion.1
Async XLA Ops:
  0.6 1.2 copy-start
  1.9 0.9 copy-start.1
  2.8 0.9 copy-start.2
